TPU v7x, 512 devices: a whole 4x8x8 slice. The times are simulated.
512 devices in a mesh: aux: 32 (over x_lo, y, core), pair: 16 (over z, x_hi).
Axes of the slice: x: 4 (x_hi: 2, x_lo: 2; x = x_hi * 2 + x_lo), y: 8, z: 8, core: 2. Of those that a mesh axis runs over, the one named last changes fastest.
Arguments:
- integrals: bfloat16 [4096, 32, 512], P('aux', 'pair'), may hold values from -0.5 to 0.5
- occ_density: bfloat16 [32, 32], replicated, may hold values from -1 to 1
- virt_density: bfloat16 [512, 512], replicated, may hold values from -0.25 to 0.25
- screen: int32 [64, 32], P('aux', 'pair'), may hold values 0 or 1
Outputs:
- polar: float32 [4096, 4096], P('aux', 'pair')
All inputs are finite; a program needn't handle non-finite values. No bound on the sum of `screen` on one device may be relied on, other than what follows from the above.
Results may differ from a plain program's by a relative error of at most 0.0041.
Values may be sent and summed in bfloat16 or wider, within the bound.
No kernel may reach another device: no remote copies, remote signals or barrier semaphores. Data moves between devices by JAX's collectives and lax.ppermute only.
A program may use at most 64 MiB of HBM per device.

v0:
```python
import jax
import jax.numpy as jnp
from jax import lax
from jax.experimental import pallas as pl
from jax.experimental.pallas import tpu as pltpu
from jax.sharding import Mesh, PartitionSpec as P


AUX = ("x_lo", "y", "core")
PAIR = ("z", "x_hi")
PLANE = ("x_lo", "core", "z", "x_hi")
WIDE = ("x_lo", "core", "x_hi")


def ring(step):
    return [(y, (y + step) % 8) for y in range(8)]


def wide_index(place, core):
    return place % 2 * 4 + core * 2 + place // 2


def x_hop():
    return [
        (wide_index(place, core), wide_index((place + 1 - 2 * core) % 4, core))
        for place in range(4)
        for core in range(2)
    ]


def prepare_kernel(screen_ref, values_ref, density_ref, out_ref, kept, virtual):
    row = lax.broadcasted_iota(jnp.int32, (256, 512), 0)
    first = jnp.where(row % 2 == 0, screen_ref[0, 0], screen_ref[0, 1])
    second = jnp.where(row % 2 == 0, screen_ref[1, 0], screen_ref[1, 1])
    keep = jnp.where(row < 128, first, second) > 0
    screened = jnp.where(keep, values_ref[...].astype(jnp.float32), 0.0)
    product = jnp.dot(screened.astype(jnp.bfloat16), density_ref[...], preferred_element_type=jnp.float32)
    for tile in range(4):
        kept[tile] = screened[:, tile * 128 : tile * 128 + 128]
        virtual[tile] = product[:, tile * 128 : tile * 128 + 128]
    for which, source in enumerate((kept, virtual)):
        for tile in range(4):
            even = source[tile, pl.ds(0, 128, stride=2), :]
            odd = source[tile, pl.ds(1, 128, stride=2), :]
            for half in range(2):
                cut = slice(half * 64, half * 64 + 64)
                block = jnp.concatenate([even[:, cut], odd[:, cut]], axis=1).astype(jnp.bfloat16)
                for w in range(8):
                    dest = w // 2 * 16 + (tile * 2 + half) * 2 + w % 2
                    out_ref[dest, which * 16 : which * 16 + 16, :] = block[w * 16 : w * 16 + 16, :]


def prepare(screen, integrals, virt_density):
    vmem = pl.BlockSpec(memory_space=pltpu.VMEM)
    return pl.pallas_call(
        prepare_kernel,
        out_shape=jax.ShapeDtypeStruct((64, 32, 128), jnp.bfloat16),
        in_specs=[pl.BlockSpec(memory_space=pltpu.SMEM), vmem, vmem],
        out_specs=vmem,
        scratch_shapes=[pltpu.VMEM((4, 256, 128), jnp.float32), pltpu.VMEM((4, 256, 128), jnp.float32)],
        compiler_params=pltpu.CompilerParams(vmem_limit_bytes=8 * 1024 * 1024),
    )(screen, integrals.reshape(256, 512), virt_density)


def unpack(got):
    return got.reshape(4, 16, 16, 128).transpose(0, 2, 1, 3).reshape(64, 2048)


def multiply_kernel(where_ref, *refs):
    columns, mine, other, (out_ref, left, right, done) = refs[:8], refs[8:12], refs[12], refs[13:]
    y, place, core = where_ref[0], where_ref[1], where_ref[2]
    copies = []

    def bring(source, target):
        copies.append(pltpu.make_async_copy(source, target, done.at[len(copies)]))
        copies[-1].start()

    for i, steps in enumerate((0, 1, 2, 3, -1, -2, -3, 4)):
        at = lax.rem(y - steps + 8, 8)
        bring(columns[i], left.at[pl.ds(pl.multiple_of(at * 64, 64), 64), :])
    sign = 1 - 2 * core
    for i, steps in enumerate((0, 1, 2, 3)):
        for near in range(2):
            step = sign * steps if near else -sign * steps
            source = lax.rem(place - step + 8, 4)
            owner = core if near else 1 - core
            at = lax.rem(source, 2) * 4 + owner * 2 + source // 2
            bring(mine[i] if near else other.at[i], right.at[:, pl.ds(pl.multiple_of(at * 16, 16), 16), :])
    for copy in copies:
        copy.wait()
    for part_id in range(2):
        part = lax.dot_general(
            left[part_id * 256 : part_id * 256 + 256, :],
            right[...].reshape(512, 2048),
            (((1,), (1,)), ((), ())),
            preferred_element_type=jnp.float32,
        ).astype(jnp.bfloat16)
        for y_column in range(4):
            for x_lo_q in range(2):
                for group in range(4):
                    row = y_column * 64 + x_lo_q * 32
                    dest = group * 16 + (x_lo_q * 4 + part_id * 2 + y_column // 2) * 2 + y_column % 2
                    out_ref[dest] = part[row : row + 32, group * 128 : group * 128 + 128]


def multiply(where, columns, mine, other):
    mine = [block.reshape(4, 16, 2048) for block in mine]
    return pl.pallas_call(
        multiply_kernel,
        out_shape=jax.ShapeDtypeStruct((64, 32, 128), jnp.bfloat16),
        in_specs=[pl.BlockSpec(memory_space=pltpu.SMEM)] + [pl.BlockSpec(memory_space=pl.ANY)] * 13,
        out_specs=pl.BlockSpec(memory_space=pltpu.VMEM),
        scratch_shapes=[
            pltpu.VMEM((512, 2048), jnp.bfloat16),
            pltpu.VMEM((4, 128, 2048), jnp.bfloat16),
            pltpu.SemaphoreType.DMA((16,)),
        ],
        compiler_params=pltpu.CompilerParams(vmem_limit_bytes=20 * 1024 * 1024),
        cost_estimate=pl.CostEstimate(flops=2 * 512 * 512 * 2048, bytes_accessed=4 << 20, transcendentals=0),
    )(where, *columns, *mine, other.reshape(4, 4, 16, 2048))


def body(integrals, occ_density, virt_density, screen):
    got = lax.all_to_all(prepare(screen, integrals, virt_density), PLANE, 0, 0, tiled=True)
    own = unpack(got[:, :16])
    core = lax.axis_index("core")
    up1 = lax.ppermute(own, "y", ring(1))
    down1 = lax.ppermute(own, "y", ring(-1))
    up2 = lax.ppermute(own, "y", ring(2))
    down2 = lax.ppermute(own, "y", ring(-2))
    up3 = lax.ppermute(up2, "y", ring(1))
    down3 = lax.ppermute(down2, "y", ring(-1))
    far = lax.ppermute(up3, "y", ring(1))
    columns = [own, up1, up2, up3, down1, down2, down3, far]
    virt_rows = unpack(got[:, 16:]).reshape(64, 32, 64)
    occupied = jnp.einsum("pms,ml->pls", virt_rows, occ_density, preferred_element_type=jnp.float32)
    occupied = lax.optimization_barrier(occupied.astype(jnp.bfloat16).reshape(64, 2048))
    mine = [occupied]
    for _ in range(3):
        mine.append(lax.ppermute(mine[-1], WIDE, x_hop()))
    other = lax.ppermute(jnp.stack(mine), "core", [(0, 1), (1, 0)])
    place = lax.axis_index("x_hi") * 2 + lax.axis_index("x_lo")
    where = jnp.stack([lax.axis_index("y"), place, core]).astype(jnp.int32)
    tiles = multiply(where, columns, mine, other)
    got = lax.all_to_all(tiles, PLANE, 0, 0, tiled=True)
    total = jnp.sum(got.reshape(2, 2, 8, 2, 2, 16, 128).astype(jnp.float32), axis=2)
    return total.transpose(5, 3, 0, 1, 2, 4).reshape(128, 256)


def solution(mesh):
    fine = Mesh(mesh.devices.reshape(2, 8, 2, 8, 2), AUX + PAIR)
    placed = (P(AUX, PAIR, None), P(), P(), P(AUX, PAIR))

    return jax.shard_map(body, mesh=fine, in_specs=placed, out_specs=P(AUX, PAIR), check_vma=False)
```

profile of v0, /device:TPU:6, one launch (start us, length us, event | category | flops | bytes accessed | tf_op | source)
XLA Modules:
  0.0 135.6 jit_solution(2516647534062219429)
XLA Ops:
  0.0 0.0 copy-start
  0.0 0.0 copy-start.1
  0.0 1.1 reshape.36.values_ref
  1.1 0.0 copy-done.1
  1.1 0.0 copy-start.2
  1.1 0.7 copy-done.2
  1.8 1.0 shard_map.46
  2.8 32.2 %all_to_all.10 = bf16[64,32,128]{2,1,0:T(8,128)(2,1)S(1)} all-to-all(bf16[64,32,128]{2,1,0:T(8,128)(2,1)S(1)} %shard_map.46), channel_id=1, replica_groups=mesh['x_lo'=2,'y'=8,'core'=2,'z'=8,'x_hi'=2] {'x_lo','core','z','x_hi'}, dimensions={0} | all-to-all | bytes 1048576 | tf_op jit(solution)/shard_map/all_to_all | solution.py:124
  35.0 0.1 copy.13
  35.1 0.2 reshape_reshape.3
  35.3 0.0 copy-done
  35.3 0.3 fusion
  35.7 0.5 reshape.40
  36.2 2.2 %collective-permute-start.7 = (bf16[64,2048]{1,0:T(8,128)(2,1)S(1)}, bf16[64,2048]{1,0:T(8,128)(2,1)S(1)}, u32[]{:S(2)}, u32[]{:S(2)}) collective-permute-start(bf16[64,2048]{1,0:T(8,128)(2,1)S(1)} %reshape.40), channel_id=1, source_target_pairs={{0,256},{16,273},{256,1},{272,16},{1,257},{17,272},{257,0},{273,17... | collective-permute-start | bytes 786440 | tf_op jit(solution)/shard_map/ppermute | solution.py:140
  38.4 6.0 %collective-permute-done.7 = bf16[64,2048]{1,0:T(8,128)(2,1)S(1)} collective-permute-done((bf16[64,2048]{1,0:T(8,128)(2,1)S(1)}, bf16[64,2048]{1,0:T(8,128)(2,1)S(1)}, u32[]{:S(2)}, u32[]{:S(2)}) %collective-permute-start.7) | collective-permute-done | bytes 262176 | tf_op jit(solution)/shard_map/ppermute | solution.py:140
  44.4 3.4 %collective-permute-start.8 = (bf16[64,2048]{1,0:T(8,128)(2,1)S(1)}, bf16[64,2048]{1,0:T(8,128)(2,1)S(1)}, u32[]{:S(2)}, u32[]{:S(2)}) collective-permute-start(bf16[64,2048]{1,0:T(8,128)(2,1)S(1)} %collective-permute-done.7), channel_id=1, source_target_pairs={{0,256},{16,273},{256,1},{272,16},{1,257},{17,272},{257,0},{273,17... | collective-permute-start | bytes 786440 | tf_op jit(solution)/shard_map/ppermute | solution.py:140
  47.8 4.8 %collective-permute-done.8 = bf16[64,2048]{1,0:T(8,128)(2,1)S(1)} collective-permute-done((bf16[64,2048]{1,0:T(8,128)(2,1)S(1)}, bf16[64,2048]{1,0:T(8,128)(2,1)S(1)}, u32[]{:S(2)}, u32[]{:S(2)}) %collective-permute-start.8) | collective-permute-done | bytes 262176 | tf_op jit(solution)/shard_map/ppermute | solution.py:140
  52.7 4.6 %collective-permute-start.9 = (bf16[64,2048]{1,0:T(8,128)(2,1)S(1)}, bf16[64,2048]{1,0:T(8,128)(2,1)S(1)}, u32[]{:S(2)}, u32[]{:S(2)}) collective-permute-start(bf16[64,2048]{1,0:T(8,128)(2,1)S(1)} %collective-permute-done.8), channel_id=1, source_target_pairs={{0,256},{16,273},{256,1},{272,16},{1,257},{17,272},{257,0},{273,17... | collective-permute-start | bytes 786440 | tf_op jit(solution)/shard_map/ppermute | solution.py:140
  57.3 3.9 %collective-permute-done.9 = bf16[64,2048]{1,0:T(8,128)(2,1)S(1)} collective-permute-done((bf16[64,2048]{1,0:T(8,128)(2,1)S(1)}, bf16[64,2048]{1,0:T(8,128)(2,1)S(1)}, u32[]{:S(2)}, u32[]{:S(2)}) %collective-permute-start.9) | collective-permute-done | bytes 262176 | tf_op jit(solution)/shard_map/ppermute | solution.py:140
  61.2 1.1 pad_maximum_fusion
  62.3 1.9 %collective-permute-start.10 = (bf16[4,64,2048]{2,1,0:T(8,128)(2,1)}, bf16[4,64,2048]{2,1,0:T(8,128)(2,1)S(1)}, u32[]{:S(2)}, u32[]{:S(2)}) collective-permute-start(bf16[4,64,2048]{2,1,0:T(8,128)(2,1)} %pad_maximum_fusion), channel_id=1, source_target_pairs={{0,16},{16,0},{1,17},{17,1},{2,18},{18,2},{3,19},{19,3},{4,20},{20... | collective-permute-start | bytes 3145736 | tf_op jit(solution)/shard_map/ppermute | solution.py:141
  64.2 0.1 copy.12
  64.3 0.1 copy.21
  64.4 4.5 %collective-permute-start.1 = (bf16[64,2048]{1,0:T(8,128)(2,1)S(1)}, bf16[64,2048]{1,0:T(8,128)(2,1)S(1)}, u32[]{:S(2)}, u32[]{:S(2)}) collective-permute-start(bf16[64,2048]{1,0:T(8,128)(2,1)S(1)} %bitcast.37), channel_id=1, source_target_pairs={{0,64},{32,96},{64,128},{96,160},{128,192},{160,224},{192,0},{224,... | collective-permute-start | bytes 786440 | tf_op jit(solution)/shard_map/ppermute | solution.py:129
  68.9 3.6 %collective-permute-start.4 = (bf16[64,2048]{1,0:T(8,128)(2,1)S(1)}, bf16[64,2048]{1,0:T(8,128)(2,1)S(1)}, u32[]{:S(2)}, u32[]{:S(2)}) collective-permute-start(bf16[64,2048]{1,0:T(8,128)(2,1)S(1)} %bitcast.38), channel_id=1, source_target_pairs={{0,192},{32,224},{64,0},{96,32},{128,64},{160,96},{192,128},{224,1... | collective-permute-start | bytes 786440 | tf_op jit(solution)/shard_map/ppermute | solution.py:130
  72.5 8.0 %collective-permute-done.1.refs_2_ = bf16[64,2048]{1,0:T(8,128)(2,1)S(1)} collective-permute-done((bf16[64,2048]{1,0:T(8,128)(2,1)S(1)}, bf16[64,2048]{1,0:T(8,128)(2,1)S(1)}, u32[]{:S(2)}, u32[]{:S(2)}) %collective-permute-start.1) | collective-permute-done | bytes 262176 | tf_op jit(solution)/shard_map/ppermute | solution.py:129
  80.4 5.7 %collective-permute-start.2 = (bf16[64,2048]{1,0:T(8,128)(2,1)S(1)}, bf16[64,2048]{1,0:T(8,128)(2,1)S(1)}, u32[]{:S(2)}, u32[]{:S(2)}) collective-permute-start(bf16[64,2048]{1,0:T(8,128)(2,1)S(1)} %collective-permute-done.1.refs_2_), channel_id=1, source_target_pairs={{0,32},{32,64},{64,96},{96,128},{128,160},{160,192},{192,224},{224... | collective-permute-start | bytes 786440 | tf_op jit(solution)/shard_map/ppermute | solution.py:131
  86.2 2.5 %collective-permute-start = (bf16[64,2048]{1,0:T(8,128)(2,1)S(1)}, bf16[64,2048]{1,0:T(8,128)(2,1)S(1)}, u32[]{:S(2)}, u32[]{:S(2)}) collective-permute-start(bf16[64,2048]{1,0:T(8,128)(2,1)S(1)} %bitcast.39), channel_id=1, source_target_pairs={{0,32},{32,64},{64,96},{96,128},{128,160},{160,192},{192,224},{224... | collective-permute-start | bytes 786440 | tf_op jit(solution)/shard_map/ppermute | solution.py:127
  88.7 4.5 %collective-permute-start.3 = (bf16[64,2048]{1,0:T(8,128)(2,1)S(1)}, bf16[64,2048]{1,0:T(8,128)(2,1)}, u32[]{:S(2)}, u32[]{:S(2)}) collective-permute-start(bf16[64,2048]{1,0:T(8,128)(2,1)S(1)} %bitcast.40), channel_id=1, source_target_pairs={{0,224},{32,0},{64,32},{96,64},{128,96},{160,128},{192,160},{224,1... | collective-permute-start | bytes 786440 | tf_op jit(solution)/shard_map/ppermute | solution.py:128
  93.2 0.0 collective-permute-done.4.refs_5_
  93.2 1.9 %collective-permute-start.5 = (bf16[64,2048]{1,0:T(8,128)(2,1)S(1)}, bf16[64,2048]{1,0:T(8,128)(2,1)}, u32[]{:S(2)}, u32[]{:S(2)}) collective-permute-start(bf16[64,2048]{1,0:T(8,128)(2,1)S(1)} %collective-permute-done.4.refs_5_), channel_id=1, source_target_pairs={{0,224},{32,0},{64,32},{96,64},{128,96},{160,128},{192,160},{224,1... | collective-permute-start | bytes 786440 | tf_op jit(solution)/shard_map/ppermute | solution.py:132
  95.2 0.0 collective-permute-done.2.refs_3_
  95.2 3.9 %collective-permute-start.6 = (bf16[64,2048]{1,0:T(8,128)(2,1)S(1)}, bf16[64,2048]{1,0:T(8,128)(2,1)}, u32[]{:S(2)}, u32[]{:S(2)}) collective-permute-start(bf16[64,2048]{1,0:T(8,128)(2,1)S(1)} %collective-permute-done.2.refs_3_), channel_id=1, source_target_pairs={{0,32},{32,64},{64,96},{96,128},{128,160},{160,192},{192,224},{224... | collective-permute-start | bytes 786440 | tf_op jit(solution)/shard_map/ppermute | solution.py:133
  99.1 0.1 pad_add_fusion.where_ref
  99.2 0.0 collective-permute-done.refs_1_
  99.2 0.7 collective-permute-done.3.refs_4_
  99.9 3.9 %collective-permute-done.5.refs_6_ = bf16[64,2048]{1,0:T(8,128)(2,1)} collective-permute-done((bf16[64,2048]{1,0:T(8,128)(2,1)S(1)}, bf16[64,2048]{1,0:T(8,128)(2,1)}, u32[]{:S(2)}, u32[]{:S(2)}) %collective-permute-start.5) | collective-permute-done | bytes 262176 | tf_op jit(solution)/shard_map/ppermute | solution.py:132
  103.8 1.7 %collective-permute-done.6.refs_7_ = bf16[64,2048]{1,0:T(8,128)(2,1)} collective-permute-done((bf16[64,2048]{1,0:T(8,128)(2,1)S(1)}, bf16[64,2048]{1,0:T(8,128)(2,1)}, u32[]{:S(2)}, u32[]{:S(2)}) %collective-permute-start.6) | collective-permute-done | bytes 262176 | tf_op jit(solution)/shard_map/ppermute | solution.py:133
  105.5 0.0 collective-permute-done.10
  105.5 3.2 %shard_map.47 = bf16[64,32,128]{2,1,0:T(8,128)(2,1)S(1)} custom-call(s32[3]{0:T(128)S(1)} %pad_add_fusion.where_ref, bf16[64,2048]{1,0:T(8,128)(2,1)S(1)} %bitcast.41, bf16[64,2048]{1,0:T(8,128)(2,1)S(1)} %collective-permute-done.refs_1_, bf16[64,2048]{1,0:T(8,128)(2,1)S(1)} %collective-permute-done.1.refs_2_, ...), custom_call_target="tpu_custom_call" | custom-call | flops 1073741824 | bytes 4194304 | tf_op jit(solution)/shard_map/pallas_call | solution.py:108
  108.7 26.0 %all_to_all.11 = bf16[64,32,128]{2,1,0:T(8,128)(2,1)S(1)} all-to-all(bf16[64,32,128]{2,1,0:T(8,128)(2,1)S(1)} %shard_map.47), channel_id=1, replica_groups=mesh['x_lo'=2,'y'=8,'core'=2,'z'=8,'x_hi'=2] {'x_lo','core','z','x_hi'}, dimensions={0} | all-to-all | bytes 1048576 | tf_op jit(solution)/shard_map/all_to_all | solution.py:145
  134.7 0.1 convert_reduce_fusion
  134.8 0.8 copy.16
  (2 shorter events, 0.0 us)
Async XLA Ops:
  0.0 35.3 %copy-start = (bf16[32,32]{1,0:T(8,128)(2,1)S(1)}, bf16[32,32]{1,0:T(8,128)(2,1)}, u32[]{:S(2)}) copy-start(bf16[32,32]{1,0:T(8,128)(2,1)} %param.5) | copy-start | bytes 6148
  0.0 1.1 copy-start.1
  1.1 0.7 copy-start.2
  36.2 8.3 %collective-permute-start.7 = (bf16[64,2048]{1,0:T(8,128)(2,1)S(1)}, bf16[64,2048]{1,0:T(8,128)(2,1)S(1)}, u32[]{:S(2)}, u32[]{:S(2)}) collective-permute-start(bf16[64,2048]{1,0:T(8,128)(2,1)S(1)} %reshape.40), channel_id=1, source_target_pairs={{0,256},{16,273},{256,1},{272,16},{1,257},{17,272},{257,0},{273,17... | collective-permute-start | bytes 786440 | tf_op jit(solution)/shard_map/ppermute | solution.py:140
  44.4 8.3 %collective-permute-start.8 = (bf16[64,2048]{1,0:T(8,128)(2,1)S(1)}, bf16[64,2048]{1,0:T(8,128)(2,1)S(1)}, u32[]{:S(2)}, u32[]{:S(2)}) collective-permute-start(bf16[64,2048]{1,0:T(8,128)(2,1)S(1)} %collective-permute-done.7), channel_id=1, source_target_pairs={{0,256},{16,273},{256,1},{272,16},{1,257},{17,272},{257,0},{273,17... | collective-permute-start | bytes 786440 | tf_op jit(solution)/shard_map/ppermute | solution.py:140
  52.7 8.5 %collective-permute-start.9 = (bf16[64,2048]{1,0:T(8,128)(2,1)S(1)}, bf16[64,2048]{1,0:T(8,128)(2,1)S(1)}, u32[]{:S(2)}, u32[]{:S(2)}) collective-permute-start(bf16[64,2048]{1,0:T(8,128)(2,1)S(1)} %collective-permute-done.8), channel_id=1, source_target_pairs={{0,256},{16,273},{256,1},{272,16},{1,257},{17,272},{257,0},{273,17... | collective-permute-start | bytes 786440 | tf_op jit(solution)/shard_map/ppermute | solution.py:140
  62.3 43.2 %collective-permute-start.10 = (bf16[4,64,2048]{2,1,0:T(8,128)(2,1)}, bf16[4,64,2048]{2,1,0:T(8,128)(2,1)S(1)}, u32[]{:S(2)}, u32[]{:S(2)}) collective-permute-start(bf16[4,64,2048]{2,1,0:T(8,128)(2,1)} %pad_maximum_fusion), channel_id=1, source_target_pairs={{0,16},{16,0},{1,17},{17,1},{2,18},{18,2},{3,19},{19,3},{4,20},{20... | collective-permute-start | bytes 3145736 | tf_op jit(solution)/shard_map/ppermute | solution.py:141
  64.4 16.1 %collective-permute-start.1 = (bf16[64,2048]{1,0:T(8,128)(2,1)S(1)}, bf16[64,2048]{1,0:T(8,128)(2,1)S(1)}, u32[]{:S(2)}, u32[]{:S(2)}) collective-permute-start(bf16[64,2048]{1,0:T(8,128)(2,1)S(1)} %bitcast.37), channel_id=1, source_target_pairs={{0,64},{32,96},{64,128},{96,160},{128,192},{160,224},{192,0},{224,... | collective-permute-start | bytes 786440 | tf_op jit(solution)/shard_map/ppermute | solution.py:129
  68.9 24.4 %collective-permute-start.4 = (bf16[64,2048]{1,0:T(8,128)(2,1)S(1)}, bf16[64,2048]{1,0:T(8,128)(2,1)S(1)}, u32[]{:S(2)}, u32[]{:S(2)}) collective-permute-start(bf16[64,2048]{1,0:T(8,128)(2,1)S(1)} %bitcast.38), channel_id=1, source_target_pairs={{0,192},{32,224},{64,0},{96,32},{128,64},{160,96},{192,128},{224,1... | collective-permute-start | bytes 786440 | tf_op jit(solution)/shard_map/ppermute | solution.py:130
  80.4 14.7 %collective-permute-start.2 = (bf16[64,2048]{1,0:T(8,128)(2,1)S(1)}, bf16[64,2048]{1,0:T(8,128)(2,1)S(1)}, u32[]{:S(2)}, u32[]{:S(2)}) collective-permute-start(bf16[64,2048]{1,0:T(8,128)(2,1)S(1)} %collective-permute-done.1.refs_2_), channel_id=1, source_target_pairs={{0,32},{32,64},{64,96},{96,128},{128,160},{160,192},{192,224},{224... | collective-permute-start | bytes 786440 | tf_op jit(solution)/shard_map/ppermute | solution.py:131
  86.2 13.0 %collective-permute-start = (bf16[64,2048]{1,0:T(8,128)(2,1)S(1)}, bf16[64,2048]{1,0:T(8,128)(2,1)S(1)}, u32[]{:S(2)}, u32[]{:S(2)}) collective-permute-start(bf16[64,2048]{1,0:T(8,128)(2,1)S(1)} %bitcast.39), channel_id=1, source_target_pairs={{0,32},{32,64},{64,96},{96,128},{128,160},{160,192},{192,224},{224... | collective-permute-start | bytes 786440 | tf_op jit(solution)/shard_map/ppermute | solution.py:127
  88.7 11.2 %collective-permute-start.3 = (bf16[64,2048]{1,0:T(8,128)(2,1)S(1)}, bf16[64,2048]{1,0:T(8,128)(2,1)}, u32[]{:S(2)}, u32[]{:S(2)}) collective-permute-start(bf16[64,2048]{1,0:T(8,128)(2,1)S(1)} %bitcast.40), channel_id=1, source_target_pairs={{0,224},{32,0},{64,32},{96,64},{128,96},{160,128},{192,160},{224,1... | collective-permute-start | bytes 786440 | tf_op jit(solution)/shard_map/ppermute | solution.py:128
  93.2 10.5 %collective-permute-start.5 = (bf16[64,2048]{1,0:T(8,128)(2,1)S(1)}, bf16[64,2048]{1,0:T(8,128)(2,1)}, u32[]{:S(2)}, u32[]{:S(2)}) collective-permute-start(bf16[64,2048]{1,0:T(8,128)(2,1)S(1)} %collective-permute-done.4.refs_5_), channel_id=1, source_target_pairs={{0,224},{32,0},{64,32},{96,64},{128,96},{160,128},{192,160},{224,1... | collective-permute-start | bytes 786440 | tf_op jit(solution)/shard_map/ppermute | solution.py:132
  95.2 10.3 %collective-permute-start.6 = (bf16[64,2048]{1,0:T(8,128)(2,1)S(1)}, bf16[64,2048]{1,0:T(8,128)(2,1)}, u32[]{:S(2)}, u32[]{:S(2)}) collective-permute-start(bf16[64,2048]{1,0:T(8,128)(2,1)S(1)} %collective-permute-done.2.refs_3_), channel_id=1, source_target_pairs={{0,32},{32,64},{64,96},{96,128},{128,160},{160,192},{192,224},{224... | collective-permute-start | bytes 786440 | tf_op jit(solution)/shard_map/ppermute | solution.py:133
where the time goes:
time: 136 us
  blocking collectives  58.2 us (43%)
  starting transfers between devices  38.9 us (29%)
  waiting for transfers between devices  29 us (21%)
  Pallas kernels  4.16 us (3%)
  local copies, waits for them, and re-layouts  3.52 us (3%)
    all_to_all x1, blocking collectives, body(): lax.all_to_all(prepare(screen, integrals, virt_density), PLANE, 0, 0, til...  32.2 us
    all_to_all x1, blocking collectives, body(): got = lax.all_to_all(tiles, PLANE, 0, 0, tiled=True)  26 us
    ppermute x3, waiting for transfers between devices, body(): mine.append(lax.ppermute(mine[-1], WIDE, x_hop()))  14.7 us
    ppermute x3, starting transfers between devices, body(): mine.append(lax.ppermute(mine[-1], WIDE, x_hop()))  10.2 us
    ppermute x1, waiting for transfers between devices, body(): up2 = lax.ppermute(own, 'y', ring(2))  7.97 us
    ppermute x1, starting transfers between devices, body(): up3 = lax.ppermute(up2, 'y', ring(1))  5.72 us
    ppermute x1, starting transfers between devices, body(): up2 = lax.ppermute(own, 'y', ring(2))  4.52 us
    ppermute x1, starting transfers between devices, body(): down1 = lax.ppermute(own, 'y', ring(-1))  4.51 us
  transfers between devices with their start and end apart: 11, of which 7 were waited for; matrix products, arithmetic and copies ran while one was open for 0% of the time, Pallas kernels for 0%

commit v1 on v0

--- a/solution.py
+++ b/solution.py
@@ -9,23 +9,11 @@
 AUX = ("x_lo", "y", "core")
 PAIR = ("z", "x_hi")
 PLANE = ("x_lo", "core", "z", "x_hi")
-WIDE = ("x_lo", "core", "x_hi")
+XX = ("x_lo", "x_hi")
 
 
 def ring(step):
     return [(y, (y + step) % 8) for y in range(8)]
-
-
-def wide_index(place, core):
-    return place % 2 * 4 + core * 2 + place // 2
-
-
-def x_hop():
-    return [
-        (wide_index(place, core), wide_index((place + 1 - 2 * core) % 4, core))
-        for place in range(4)
-        for core in range(2)
-    ]
 
 
 def prepare_kernel(screen_ref, values_ref, density_ref, out_ref, kept, virtual):
@@ -67,8 +55,8 @@
 
 
 def multiply_kernel(where_ref, *refs):
-    columns, mine, other, (out_ref, left, right, done) = refs[:8], refs[8:12], refs[12], refs[13:]
-    y, place, core = where_ref[0], where_ref[1], where_ref[2]
+    columns, mine, other, (out_ref, left, right, done) = refs[:8], refs[8], refs[9], refs[10:]
+    y, core = where_ref[0], where_ref[1]
     copies = []
 
     def bring(source, target):
@@ -78,14 +66,10 @@
     for i, steps in enumerate((0, 1, 2, 3, -1, -2, -3, 4)):
         at = lax.rem(y - steps + 8, 8)
         bring(columns[i], left.at[pl.ds(pl.multiple_of(at * 64, 64), 64), :])
-    sign = 1 - 2 * core
-    for i, steps in enumerate((0, 1, 2, 3)):
-        for near in range(2):
-            step = sign * steps if near else -sign * steps
-            source = lax.rem(place - step + 8, 4)
-            owner = core if near else 1 - core
-            at = lax.rem(source, 2) * 4 + owner * 2 + source // 2
-            bring(mine[i] if near else other.at[i], right.at[:, pl.ds(pl.multiple_of(at * 16, 16), 16), :])
+    for i in range(4):
+        for blocks, owner in ((mine, core), (other, 1 - core)):
+            at = i // 2 * 4 + owner * 2 + i % 2
+            bring(blocks.at[i], right.at[:, pl.ds(pl.multiple_of(at * 16, 16), 16), :])
     for copy in copies:
         copy.wait()
     for part_id in range(2):
@@ -104,11 +88,10 @@
 
 
 def multiply(where, columns, mine, other):
-    mine = [block.reshape(4, 16, 2048) for block in mine]
     return pl.pallas_call(
         multiply_kernel,
         out_shape=jax.ShapeDtypeStruct((64, 32, 128), jnp.bfloat16),
-        in_specs=[pl.BlockSpec(memory_space=pltpu.SMEM)] + [pl.BlockSpec(memory_space=pl.ANY)] * 13,
+        in_specs=[pl.BlockSpec(memory_space=pltpu.SMEM)] + [pl.BlockSpec(memory_space=pl.ANY)] * 10,
         out_specs=pl.BlockSpec(memory_space=pltpu.VMEM),
         scratch_shapes=[
             pltpu.VMEM((512, 2048), jnp.bfloat16),
@@ -117,7 +100,7 @@
         ],
         compiler_params=pltpu.CompilerParams(vmem_limit_bytes=20 * 1024 * 1024),
         cost_estimate=pl.CostEstimate(flops=2 * 512 * 512 * 2048, bytes_accessed=4 << 20, transcendentals=0),
-    )(where, *columns, *mine, other.reshape(4, 4, 16, 2048))
+    )(where, *columns, mine.reshape(4, 4, 16, 2048), other.reshape(4, 4, 16, 2048))
 
 
 def body(integrals, occ_density, virt_density, screen):
@@ -135,12 +118,9 @@
     virt_rows = unpack(got[:, 16:]).reshape(64, 32, 64)
     occupied = jnp.einsum("pms,ml->pls", virt_rows, occ_density, preferred_element_type=jnp.float32)
     occupied = lax.optimization_barrier(occupied.astype(jnp.bfloat16).reshape(64, 2048))
-    mine = [occupied]
-    for _ in range(3):
-        mine.append(lax.ppermute(mine[-1], WIDE, x_hop()))
-    other = lax.ppermute(jnp.stack(mine), "core", [(0, 1), (1, 0)])
-    place = lax.axis_index("x_hi") * 2 + lax.axis_index("x_lo")
-    where = jnp.stack([lax.axis_index("y"), place, core]).astype(jnp.int32)
+    mine = lax.all_to_all(jnp.broadcast_to(occupied, (4, 64, 2048)), XX, 0, 0, tiled=True)
+    other = lax.ppermute(mine, "core", [(0, 1), (1, 0)])
+    where = jnp.stack([lax.axis_index("y"), core]).astype(jnp.int32)
     tiles = multiply(where, columns, mine, other)
     got = lax.all_to_all(tiles, PLANE, 0, 0, tiled=True)
     total = jnp.sum(got.reshape(2, 2, 8, 2, 2, 16, 128).astype(jnp.float32), axis=2)

time: 136 us -> 126 us (0.926)
  blocking collectives: 58.2 us -> 73.2 us
  waiting for transfers between devices: 29 us -> 16.1 us
  starting transfers between devices: 38.9 us -> 27.4 us
    all_to_all x0 -> x1, blocking collectives: none -> 16.2 us  [body(): lax.all_to_all(jnp.broadcast_to(occupied, (4, 64, 2048)), XX, 0, 0, tiled...]
    ppermute x4 -> x1, waiting for transfers between devices: 14.8 us -> 0.01 us  [body(): other = lax.ppermute(mine, 'core', [(0, 1), (1, 0)])]
    ppermute x4 -> x1, starting transfers between devices: 12.2 us -> 1.91 us  [body(): other = lax.ppermute(mine, 'core', [(0, 1), (1, 0)])]
    ppermute x1, waiting for transfers between devices: 1.69 us -> 4.73 us  [body(): far = lax.ppermute(up3, 'y', ring(1))]
    ppermute x1, waiting for transfers between devices: 3.87 us -> 1.8 us  [body(): down3 = lax.ppermute(down2, 'y', ring(-1))]
    ppermute x1, starting transfers between devices: 1.92 us -> 3.88 us  [body(): down3 = lax.ppermute(down2, 'y', ring(-1))]
    ppermute x1, starting transfers between devices: 3.92 us -> 1.97 us  [body(): far = lax.ppermute(up3, 'y', ring(1))]
    ppermute x1, starting transfers between devices: 4.51 us -> 2.67 us  [body(): down1 = lax.ppermute(own, 'y', ring(-1))]
  transfers between devices with their start and end apart: 11 -> 8, of which waited for: 7 -> 4; matrix products, arithmetic and copies ran while one was open for 0% -> 0% of each run, Pallas kernels for 0% -> 0%
where the time goes in v1:
time: 126 us; the launch traced here: 125 us
  blocking collectives  73.2 us (58%)
  starting transfers between devices  27.4 us (22%)
  waiting for transfers between devices  16.1 us (13%)
  Pallas kernels  4.12 us (3%)
  local copies, waits for them, and re-layouts  3.64 us (3%)
    all_to_all x1, blocking collectives, body(): lax.all_to_all(prepare(screen, integrals, virt_density), PLANE, 0, 0, til...  32.2 us
    all_to_all x1, blocking collectives, body(): got = lax.all_to_all(tiles, PLANE, 0, 0, tiled=True)  24.8 us
    all_to_all x1, blocking collectives, body(): lax.all_to_all(jnp.broadcast_to(occupied, (4, 64, 2048)), XX, 0, 0, tiled...  16.2 us
    ppermute x1, waiting for transfers between devices, body(): up2 = lax.ppermute(own, 'y', ring(2))  7.98 us
    ppermute x1, starting transfers between devices, body(): up3 = lax.ppermute(up2, 'y', ring(1))  5.71 us
    ppermute x1, waiting for transfers between devices, body(): far = lax.ppermute(up3, 'y', ring(1))  4.73 us
    ppermute x1, starting transfers between devices, body(): up2 = lax.ppermute(own, 'y', ring(2))  4.52 us
    ppermute x1, starting transfers between devices, body(): down3 = lax.ppermute(down2, 'y', ring(-1))  3.88 us
  transfers between devices with their start and end apart: 8, of which 4 were waited for; matrix products, arithmetic and copies ran while one was open for 0% of the time, Pallas kernels for 0%

profile of v1, /device:TPU:6, one launch (start us, length us, event | category | flops | bytes accessed | tf_op | source)
XLA Modules:
  0.0 125.2 jit_solution(14641686887751159090)
XLA Ops:
  0.0 0.0 copy-start
  0.0 0.0 copy-start.1
  0.0 1.1 reshape.27.values_ref
  1.1 0.0 copy-done.1
  1.1 0.0 copy-start.2
  1.1 0.7 copy-done.2
  1.8 1.0 shard_map.46
  2.8 32.2 %all_to_all.15 = bf16[64,32,128]{2,1,0:T(8,128)(2,1)S(1)} all-to-all(bf16[64,32,128]{2,1,0:T(8,128)(2,1)S(1)} %shard_map.46), channel_id=1, replica_groups=mesh['x_lo'=2,'y'=8,'core'=2,'z'=8,'x_hi'=2] {'x_lo','core','z','x_hi'}, dimensions={0} | all-to-all | bytes 1048576 | tf_op jit(solution)/shard_map/all_to_all | solution.py:107
  35.0 0.1 copy.13
  35.1 0.2 reshape_reshape.3
  35.3 0.0 copy-done
  35.3 0.3 fusion
  35.7 0.5 reshape.31
  36.2 0.1 broadcast_in_dim.3
  36.3 16.2 %all_to_all.16 = bf16[4,64,2048]{2,1,0:T(8,128)(2,1)S(1)} all-to-all(bf16[4,64,2048]{2,1,0:T(8,128)(2,1)S(1)} %broadcast_in_dim.3), channel_id=1, replica_groups=mesh['x_lo'=2,'y'=8,'core'=2,'z'=8,'x_hi'=2] {'x_lo','x_hi'}, dimensions={0} | all-to-all | bytes 2097152 | tf_op jit(solution)/shard_map/all_to_all | solution.py:121
  52.4 1.9 %collective-permute-start.7 = (bf16[4,64,2048]{2,1,0:T(8,128)(2,1)S(1)}, bf16[4,64,2048]{2,1,0:T(8,128)(2,1)S(1)}, u32[]{:S(2)}, u32[]{:S(2)}) collective-permute-start(bf16[4,64,2048]{2,1,0:T(8,128)(2,1)S(1)} %all_to_all.16), channel_id=1, source_target_pairs={{0,16},{16,0},{1,17},{17,1},{2,18},{18,2},{3,19},{19,3},{4,20},{20... | collective-permute-start | bytes 3145736 | tf_op jit(solution)/shard_map/ppermute | solution.py:122
  54.4 0.1 copy.12
  54.4 0.1 copy.21
  54.5 4.5 %collective-permute-start.1 = (bf16[64,2048]{1,0:T(8,128)(2,1)S(1)}, bf16[64,2048]{1,0:T(8,128)(2,1)S(1)}, u32[]{:S(2)}, u32[]{:S(2)}) collective-permute-start(bf16[64,2048]{1,0:T(8,128)(2,1)S(1)} %bitcast.28), channel_id=1, source_target_pairs={{0,64},{32,96},{64,128},{96,160},{128,192},{160,224},{192,0},{224,... | collective-permute-start | bytes 786440 | tf_op jit(solution)/shard_map/ppermute | solution.py:112
  59.0 3.6 %collective-permute-start.4 = (bf16[64,2048]{1,0:T(8,128)(2,1)S(1)}, bf16[64,2048]{1,0:T(8,128)(2,1)S(1)}, u32[]{:S(2)}, u32[]{:S(2)}) collective-permute-start(bf16[64,2048]{1,0:T(8,128)(2,1)S(1)} %bitcast.29), channel_id=1, source_target_pairs={{0,192},{32,224},{64,0},{96,32},{128,64},{160,96},{192,128},{224,1... | collective-permute-start | bytes 786440 | tf_op jit(solution)/shard_map/ppermute | solution.py:113
  62.6 8.0 %collective-permute-done.1.refs_2_ = bf16[64,2048]{1,0:T(8,128)(2,1)S(1)} collective-permute-done((bf16[64,2048]{1,0:T(8,128)(2,1)S(1)}, bf16[64,2048]{1,0:T(8,128)(2,1)S(1)}, u32[]{:S(2)}, u32[]{:S(2)}) %collective-permute-start.1) | collective-permute-done | bytes 262176 | tf_op jit(solution)/shard_map/ppermute | solution.py:112
  70.6 5.7 %collective-permute-start.2 = (bf16[64,2048]{1,0:T(8,128)(2,1)S(1)}, bf16[64,2048]{1,0:T(8,128)(2,1)S(1)}, u32[]{:S(2)}, u32[]{:S(2)}) collective-permute-start(bf16[64,2048]{1,0:T(8,128)(2,1)S(1)} %collective-permute-done.1.refs_2_), channel_id=1, source_target_pairs={{0,32},{32,64},{64,96},{96,128},{128,160},{160,192},{192,224},{224... | collective-permute-start | bytes 786440 | tf_op jit(solution)/shard_map/ppermute | solution.py:114
  76.3 2.7 %collective-permute-start.3 = (bf16[64,2048]{1,0:T(8,128)(2,1)S(1)}, bf16[64,2048]{1,0:T(8,128)(2,1)S(1)}, u32[]{:S(2)}, u32[]{:S(2)}) collective-permute-start(bf16[64,2048]{1,0:T(8,128)(2,1)S(1)} %bitcast.30), channel_id=1, source_target_pairs={{0,224},{32,0},{64,32},{96,64},{128,96},{160,128},{192,160},{224,1... | collective-permute-start | bytes 786440 | tf_op jit(solution)/shard_map/ppermute | solution.py:111
  79.0 3.2 %collective-permute-start = (bf16[64,2048]{1,0:T(8,128)(2,1)S(1)}, bf16[64,2048]{1,0:T(8,128)(2,1)}, u32[]{:S(2)}, u32[]{:S(2)}) collective-permute-start(bf16[64,2048]{1,0:T(8,128)(2,1)S(1)} %bitcast.31), channel_id=1, source_target_pairs={{0,32},{32,64},{64,96},{96,128},{128,160},{160,192},{192,224},{224... | collective-permute-start | bytes 786440 | tf_op jit(solution)/shard_map/ppermute | solution.py:110
  82.2 0.0 collective-permute-done.4.refs_5_
  82.2 3.9 %collective-permute-start.5 = (bf16[64,2048]{1,0:T(8,128)(2,1)S(1)}, bf16[64,2048]{1,0:T(8,128)(2,1)}, u32[]{:S(2)}, u32[]{:S(2)}) collective-permute-start(bf16[64,2048]{1,0:T(8,128)(2,1)S(1)} %collective-permute-done.4.refs_5_), channel_id=1, source_target_pairs={{0,224},{32,0},{64,32},{96,64},{128,96},{160,128},{192,160},{224,1... | collective-permute-start | bytes 786440 | tf_op jit(solution)/shard_map/ppermute | solution.py:115
  86.1 0.0 collective-permute-done.2.refs_3_
  86.1 2.0 %collective-permute-start.6 = (bf16[64,2048]{1,0:T(8,128)(2,1)S(1)}, bf16[64,2048]{1,0:T(8,128)(2,1)}, u32[]{:S(2)}, u32[]{:S(2)}) collective-permute-start(bf16[64,2048]{1,0:T(8,128)(2,1)S(1)} %collective-permute-done.2.refs_3_), channel_id=1, source_target_pairs={{0,32},{32,64},{64,96},{96,128},{128,160},{160,192},{192,224},{224... | collective-permute-start | bytes 786440 | tf_op jit(solution)/shard_map/ppermute | solution.py:116
  88.1 0.1 pad_add_fusion.where_ref
  88.1 0.0 collective-permute-done.3.refs_4_
  88.1 1.6 %collective-permute-done.refs_1_ = bf16[64,2048]{1,0:T(8,128)(2,1)} collective-permute-done((bf16[64,2048]{1,0:T(8,128)(2,1)S(1)}, bf16[64,2048]{1,0:T(8,128)(2,1)}, u32[]{:S(2)}, u32[]{:S(2)}) %collective-permute-start) | collective-permute-done | bytes 262176 | tf_op jit(solution)/shard_map/ppermute | solution.py:110
  89.8 1.8 %collective-permute-done.5.refs_6_ = bf16[64,2048]{1,0:T(8,128)(2,1)} collective-permute-done((bf16[64,2048]{1,0:T(8,128)(2,1)S(1)}, bf16[64,2048]{1,0:T(8,128)(2,1)}, u32[]{:S(2)}, u32[]{:S(2)}) %collective-permute-start.5) | collective-permute-done | bytes 262176 | tf_op jit(solution)/shard_map/ppermute | solution.py:115
  91.6 4.7 %collective-permute-done.6.refs_7_ = bf16[64,2048]{1,0:T(8,128)(2,1)} collective-permute-done((bf16[64,2048]{1,0:T(8,128)(2,1)S(1)}, bf16[64,2048]{1,0:T(8,128)(2,1)}, u32[]{:S(2)}, u32[]{:S(2)}) %collective-permute-start.6) | collective-permute-done | bytes 262176 | tf_op jit(solution)/shard_map/ppermute | solution.py:116
  96.3 0.0 collective-permute-done.7
  96.3 3.2 %shard_map.47 = bf16[64,32,128]{2,1,0:T(8,128)(2,1)S(1)} custom-call(s32[2]{0:T(128)S(1)} %pad_add_fusion.where_ref, bf16[64,2048]{1,0:T(8,128)(2,1)S(1)} %bitcast.32, bf16[64,2048]{1,0:T(8,128)(2,1)} %collective-permute-done.refs_1_, bf16[64,2048]{1,0:T(8,128)(2,1)S(1)} %collective-permute-done.1.refs_2_, ...), custom_call_target="tpu_custom_call" | custom-call | flops 1073741824 | bytes 4194304 | tf_op jit(solution)/shard_map/pallas_call | solution.py:91
  99.5 24.8 %all_to_all.17 = bf16[64,32,128]{2,1,0:T(8,128)(2,1)S(1)} all-to-all(bf16[64,32,128]{2,1,0:T(8,128)(2,1)S(1)} %shard_map.47), channel_id=1, replica_groups=mesh['x_lo'=2,'y'=8,'core'=2,'z'=8,'x_hi'=2] {'x_lo','core','z','x_hi'}, dimensions={0} | all-to-all | bytes 1048576 | tf_op jit(solution)/shard_map/all_to_all | solution.py:125
  124.3 0.1 convert_reduce_fusion
  124.4 0.8 copy.16
  (2 shorter events, 0.0 us)
Async XLA Ops:
  0.0 35.3 %copy-start = (bf16[32,32]{1,0:T(8,128)(2,1)S(1)}, bf16[32,32]{1,0:T(8,128)(2,1)}, u32[]{:S(2)}) copy-start(bf16[32,32]{1,0:T(8,128)(2,1)} %param.5) | copy-start | bytes 6148
  0.0 1.1 copy-start.1
  1.1 0.7 copy-start.2
  52.4 43.9 %collective-permute-start.7 = (bf16[4,64,2048]{2,1,0:T(8,128)(2,1)S(1)}, bf16[4,64,2048]{2,1,0:T(8,128)(2,1)S(1)}, u32[]{:S(2)}, u32[]{:S(2)}) collective-permute-start(bf16[4,64,2048]{2,1,0:T(8,128)(2,1)S(1)} %all_to_all.16), channel_id=1, source_target_pairs={{0,16},{16,0},{1,17},{17,1},{2,18},{18,2},{3,19},{19,3},{4,20},{20... | collective-permute-start | bytes 3145736 | tf_op jit(solution)/shard_map/ppermute | solution.py:122
  54.5 16.1 %collective-permute-start.1 = (bf16[64,2048]{1,0:T(8,128)(2,1)S(1)}, bf16[64,2048]{1,0:T(8,128)(2,1)S(1)}, u32[]{:S(2)}, u32[]{:S(2)}) collective-permute-start(bf16[64,2048]{1,0:T(8,128)(2,1)S(1)} %bitcast.28), channel_id=1, source_target_pairs={{0,64},{32,96},{64,128},{96,160},{128,192},{160,224},{192,0},{224,... | collective-permute-start | bytes 786440 | tf_op jit(solution)/shard_map/ppermute | solution.py:112
  59.0 23.1 %collective-permute-start.4 = (bf16[64,2048]{1,0:T(8,128)(2,1)S(1)}, bf16[64,2048]{1,0:T(8,128)(2,1)S(1)}, u32[]{:S(2)}, u32[]{:S(2)}) collective-permute-start(bf16[64,2048]{1,0:T(8,128)(2,1)S(1)} %bitcast.29), channel_id=1, source_target_pairs={{0,192},{32,224},{64,0},{96,32},{128,64},{160,96},{192,128},{224,1... | collective-permute-start | bytes 786440 | tf_op jit(solution)/shard_map/ppermute | solution.py:113
  70.6 15.5 %collective-permute-start.2 = (bf16[64,2048]{1,0:T(8,128)(2,1)S(1)}, bf16[64,2048]{1,0:T(8,128)(2,1)S(1)}, u32[]{:S(2)}, u32[]{:S(2)}) collective-permute-start(bf16[64,2048]{1,0:T(8,128)(2,1)S(1)} %collective-permute-done.1.refs_2_), channel_id=1, source_target_pairs={{0,32},{32,64},{64,96},{96,128},{128,160},{160,192},{192,224},{224... | collective-permute-start | bytes 786440 | tf_op jit(solution)/shard_map/ppermute | solution.py:114
  76.3 11.8 %collective-permute-start.3 = (bf16[64,2048]{1,0:T(8,128)(2,1)S(1)}, bf16[64,2048]{1,0:T(8,128)(2,1)S(1)}, u32[]{:S(2)}, u32[]{:S(2)}) collective-permute-start(bf16[64,2048]{1,0:T(8,128)(2,1)S(1)} %bitcast.30), channel_id=1, source_target_pairs={{0,224},{32,0},{64,32},{96,64},{128,96},{160,128},{192,160},{224,1... | collective-permute-start | bytes 786440 | tf_op jit(solution)/shard_map/ppermute | solution.py:111
  79.0 10.8 %collective-permute-start = (bf16[64,2048]{1,0:T(8,128)(2,1)S(1)}, bf16[64,2048]{1,0:T(8,128)(2,1)}, u32[]{:S(2)}, u32[]{:S(2)}) collective-permute-start(bf16[64,2048]{1,0:T(8,128)(2,1)S(1)} %bitcast.31), channel_id=1, source_target_pairs={{0,32},{32,64},{64,96},{96,128},{128,160},{160,192},{192,224},{224... | collective-permute-start | bytes 786440 | tf_op jit(solution)/shard_map/ppermute | solution.py:110
  82.2 9.4 %collective-permute-start.5 = (bf16[64,2048]{1,0:T(8,128)(2,1)S(1)}, bf16[64,2048]{1,0:T(8,128)(2,1)}, u32[]{:S(2)}, u32[]{:S(2)}) collective-permute-start(bf16[64,2048]{1,0:T(8,128)(2,1)S(1)} %collective-permute-done.4.refs_5_), channel_id=1, source_target_pairs={{0,224},{32,0},{64,32},{96,64},{128,96},{160,128},{192,160},{224,1... | collective-permute-start | bytes 786440 | tf_op jit(solution)/shard_map/ppermute | solution.py:115
  86.1 10.2 %collective-permute-start.6 = (bf16[64,2048]{1,0:T(8,128)(2,1)S(1)}, bf16[64,2048]{1,0:T(8,128)(2,1)}, u32[]{:S(2)}, u32[]{:S(2)}) collective-permute-start(bf16[64,2048]{1,0:T(8,128)(2,1)S(1)} %collective-permute-done.2.refs_3_), channel_id=1, source_target_pairs={{0,32},{32,64},{64,96},{96,128},{128,160},{160,192},{192,224},{224... | collective-permute-start | bytes 786440 | tf_op jit(solution)/shard_map/ppermute | solution.py:116

commit v2 on v1

--- a/solution.py
+++ b/solution.py
@@ -103,6 +103,30 @@
     )(where, *columns, mine.reshape(4, 4, 16, 2048), other.reshape(4, 4, 16, 2048))
 
 
+def finish_kernel(tiles_ref, out_ref):
+    for core_q in range(2):
+        rows = pl.ds(core_q * 16, 16)
+        parts = []
+        for w in range(8):
+            total = None
+            for z in range(8):
+                part = tiles_ref[w // 2 * 16 + z * 2 + w % 2, rows, :].astype(jnp.float32)
+                total = part if total is None else total + part
+            parts.append(total)
+        out_ref[:, core_q * 128 : core_q * 128 + 128] = jnp.concatenate(parts, axis=0).T
+
+
+def finish(tiles):
+    vmem = pl.BlockSpec(memory_space=pltpu.VMEM)
+    return pl.pallas_call(
+        finish_kernel,
+        out_shape=jax.ShapeDtypeStruct((128, 256), jnp.float32),
+        in_specs=[vmem],
+        out_specs=vmem,
+        compiler_params=pltpu.CompilerParams(vmem_limit_bytes=8 * 1024 * 1024),
+    )(tiles)
+
+
 def body(integrals, occ_density, virt_density, screen):
     got = lax.all_to_all(prepare(screen, integrals, virt_density), PLANE, 0, 0, tiled=True)
     own = unpack(got[:, :16])
@@ -123,8 +147,7 @@
     where = jnp.stack([lax.axis_index("y"), core]).astype(jnp.int32)
     tiles = multiply(where, columns, mine, other)
     got = lax.all_to_all(tiles, PLANE, 0, 0, tiled=True)
-    total = jnp.sum(got.reshape(2, 2, 8, 2, 2, 16, 128).astype(jnp.float32), axis=2)
-    return total.transpose(5, 3, 0, 1, 2, 4).reshape(128, 256)
+    return finish(got)
 
 
 def solution(mesh):

time: 126 us -> 126 us (level)
  no operation moved by 1% of the time
where the time goes in v2:
time: 126 us; the launch traced here: 125 us
  blocking collectives  73.2 us (58%)
  starting transfers between devices  27.4 us (22%)
  waiting for transfers between devices  16.1 us (13%)
  Pallas kernels  4.91 us (4%)
  local copies, waits for them, and re-layouts  2.88 us (2%)
    all_to_all x1, blocking collectives, body(): lax.all_to_all(prepare(screen, integrals, virt_density), PLANE, 0, 0, til...  32.2 us
    all_to_all x1, blocking collectives, body(): got = lax.all_to_all(tiles, PLANE, 0, 0, tiled=True)  24.8 us
    all_to_all x1, blocking collectives, body(): lax.all_to_all(jnp.broadcast_to(occupied, (4, 64, 2048)), XX, 0, 0, tiled...  16.2 us
    ppermute x1, waiting for transfers between devices, body(): up2 = lax.ppermute(own, 'y', ring(2))  7.98 us
    ppermute x1, starting transfers between devices, body(): up3 = lax.ppermute(up2, 'y', ring(1))  5.71 us
    ppermute x1, waiting for transfers between devices, body(): far = lax.ppermute(up3, 'y', ring(1))  4.73 us
    ppermute x1, starting transfers between devices, body(): up2 = lax.ppermute(own, 'y', ring(2))  4.52 us
    ppermute x1, starting transfers between devices, body(): down3 = lax.ppermute(down2, 'y', ring(-1))  3.88 us
  transfers between devices with their start and end apart: 8, of which 4 were waited for; matrix products, arithmetic and copies ran while one was open for 0% of the time, Pallas kernels for 0%

profile of v2, /device:TPU:6, one launch (start us, length us, event | category | flops | bytes accessed | tf_op | source)
XLA Modules:
  0.0 125.1 jit_solution(1798808666191850663)
XLA Ops:
  0.0 0.0 copy-start
  0.0 0.0 copy-start.1
  0.0 1.1 reshape.21.values_ref
  1.1 0.0 copy-done.1
  1.1 0.0 copy-start.2
  1.1 0.7 copy-done.2
  1.8 1.0 shard_map.46
  2.8 32.2 %all_to_all.15 = bf16[64,32,128]{2,1,0:T(8,128)(2,1)S(1)} all-to-all(bf16[64,32,128]{2,1,0:T(8,128)(2,1)S(1)} %shard_map.46), channel_id=1, replica_groups=mesh['x_lo'=2,'y'=8,'core'=2,'z'=8,'x_hi'=2] {'x_lo','core','z','x_hi'}, dimensions={0} | all-to-all | bytes 1048576 | tf_op jit(solution)/shard_map/all_to_all | solution.py:131
  35.0 0.1 copy.6
  35.1 0.2 reshape_reshape.3
  35.3 0.0 copy-done
  35.3 0.3 fusion
  35.7 0.5 reshape.25
  36.2 0.1 broadcast_in_dim.3
  36.3 16.2 %all_to_all.16 = bf16[4,64,2048]{2,1,0:T(8,128)(2,1)S(1)} all-to-all(bf16[4,64,2048]{2,1,0:T(8,128)(2,1)S(1)} %broadcast_in_dim.3), channel_id=1, replica_groups=mesh['x_lo'=2,'y'=8,'core'=2,'z'=8,'x_hi'=2] {'x_lo','x_hi'}, dimensions={0} | all-to-all | bytes 2097152 | tf_op jit(solution)/shard_map/all_to_all | solution.py:145
  52.4 1.9 %collective-permute-start.7 = (bf16[4,64,2048]{2,1,0:T(8,128)(2,1)S(1)}, bf16[4,64,2048]{2,1,0:T(8,128)(2,1)S(1)}, u32[]{:S(2)}, u32[]{:S(2)}) collective-permute-start(bf16[4,64,2048]{2,1,0:T(8,128)(2,1)S(1)} %all_to_all.16), channel_id=1, source_target_pairs={{0,16},{16,0},{1,17},{17,1},{2,18},{18,2},{3,19},{19,3},{4,20},{20... | collective-permute-start | bytes 3145736 | tf_op jit(solution)/shard_map/ppermute | solution.py:146
  54.4 0.1 copy.5
  54.4 0.1 copy.12
  54.5 4.5 %collective-permute-start.1 = (bf16[64,2048]{1,0:T(8,128)(2,1)S(1)}, bf16[64,2048]{1,0:T(8,128)(2,1)S(1)}, u32[]{:S(2)}, u32[]{:S(2)}) collective-permute-start(bf16[64,2048]{1,0:T(8,128)(2,1)S(1)} %bitcast.24), channel_id=1, source_target_pairs={{0,64},{32,96},{64,128},{96,160},{128,192},{160,224},{192,0},{224,... | collective-permute-start | bytes 786440 | tf_op jit(solution)/shard_map/ppermute | solution.py:136
  59.0 3.6 %collective-permute-start.4 = (bf16[64,2048]{1,0:T(8,128)(2,1)S(1)}, bf16[64,2048]{1,0:T(8,128)(2,1)S(1)}, u32[]{:S(2)}, u32[]{:S(2)}) collective-permute-start(bf16[64,2048]{1,0:T(8,128)(2,1)S(1)} %bitcast.25), channel_id=1, source_target_pairs={{0,192},{32,224},{64,0},{96,32},{128,64},{160,96},{192,128},{224,1... | collective-permute-start | bytes 786440 | tf_op jit(solution)/shard_map/ppermute | solution.py:137
  62.6 8.0 %collective-permute-done.1.refs_2_ = bf16[64,2048]{1,0:T(8,128)(2,1)S(1)} collective-permute-done((bf16[64,2048]{1,0:T(8,128)(2,1)S(1)}, bf16[64,2048]{1,0:T(8,128)(2,1)S(1)}, u32[]{:S(2)}, u32[]{:S(2)}) %collective-permute-start.1) | collective-permute-done | bytes 262176 | tf_op jit(solution)/shard_map/ppermute | solution.py:136
  70.6 5.7 %collective-permute-start.2 = (bf16[64,2048]{1,0:T(8,128)(2,1)S(1)}, bf16[64,2048]{1,0:T(8,128)(2,1)S(1)}, u32[]{:S(2)}, u32[]{:S(2)}) collective-permute-start(bf16[64,2048]{1,0:T(8,128)(2,1)S(1)} %collective-permute-done.1.refs_2_), channel_id=1, source_target_pairs={{0,32},{32,64},{64,96},{96,128},{128,160},{160,192},{192,224},{224... | collective-permute-start | bytes 786440 | tf_op jit(solution)/shard_map/ppermute | solution.py:138
  76.3 2.7 %collective-permute-start.3 = (bf16[64,2048]{1,0:T(8,128)(2,1)S(1)}, bf16[64,2048]{1,0:T(8,128)(2,1)S(1)}, u32[]{:S(2)}, u32[]{:S(2)}) collective-permute-start(bf16[64,2048]{1,0:T(8,128)(2,1)S(1)} %bitcast.26), channel_id=1, source_target_pairs={{0,224},{32,0},{64,32},{96,64},{128,96},{160,128},{192,160},{224,1... | collective-permute-start | bytes 786440 | tf_op jit(solution)/shard_map/ppermute | solution.py:135
  79.0 3.2 %collective-permute-start = (bf16[64,2048]{1,0:T(8,128)(2,1)S(1)}, bf16[64,2048]{1,0:T(8,128)(2,1)}, u32[]{:S(2)}, u32[]{:S(2)}) collective-permute-start(bf16[64,2048]{1,0:T(8,128)(2,1)S(1)} %bitcast.27), channel_id=1, source_target_pairs={{0,32},{32,64},{64,96},{96,128},{128,160},{160,192},{192,224},{224... | collective-permute-start | bytes 786440 | tf_op jit(solution)/shard_map/ppermute | solution.py:134
  82.2 0.0 collective-permute-done.4.refs_5_
  82.2 3.9 %collective-permute-start.5 = (bf16[64,2048]{1,0:T(8,128)(2,1)S(1)}, bf16[64,2048]{1,0:T(8,128)(2,1)}, u32[]{:S(2)}, u32[]{:S(2)}) collective-permute-start(bf16[64,2048]{1,0:T(8,128)(2,1)S(1)} %collective-permute-done.4.refs_5_), channel_id=1, source_target_pairs={{0,224},{32,0},{64,32},{96,64},{128,96},{160,128},{192,160},{224,1... | collective-permute-start | bytes 786440 | tf_op jit(solution)/shard_map/ppermute | solution.py:139
  86.1 0.0 collective-permute-done.2.refs_3_
  86.1 2.0 %collective-permute-start.6 = (bf16[64,2048]{1,0:T(8,128)(2,1)S(1)}, bf16[64,2048]{1,0:T(8,128)(2,1)}, u32[]{:S(2)}, u32[]{:S(2)}) collective-permute-start(bf16[64,2048]{1,0:T(8,128)(2,1)S(1)} %collective-permute-done.2.refs_3_), channel_id=1, source_target_pairs={{0,32},{32,64},{64,96},{96,128},{128,160},{160,192},{192,224},{224... | collective-permute-start | bytes 786440 | tf_op jit(solution)/shard_map/ppermute | solution.py:140
  88.1 0.1 pad_add_fusion.where_ref
  88.1 0.0 collective-permute-done.3.refs_4_
  88.1 1.6 %collective-permute-done.refs_1_ = bf16[64,2048]{1,0:T(8,128)(2,1)} collective-permute-done((bf16[64,2048]{1,0:T(8,128)(2,1)S(1)}, bf16[64,2048]{1,0:T(8,128)(2,1)}, u32[]{:S(2)}, u32[]{:S(2)}) %collective-permute-start) | collective-permute-done | bytes 262176 | tf_op jit(solution)/shard_map/ppermute | solution.py:134
  89.8 1.8 %collective-permute-done.5.refs_6_ = bf16[64,2048]{1,0:T(8,128)(2,1)} collective-permute-done((bf16[64,2048]{1,0:T(8,128)(2,1)S(1)}, bf16[64,2048]{1,0:T(8,128)(2,1)}, u32[]{:S(2)}, u32[]{:S(2)}) %collective-permute-start.5) | collective-permute-done | bytes 262176 | tf_op jit(solution)/shard_map/ppermute | solution.py:139
  91.6 4.7 %collective-permute-done.6.refs_7_ = bf16[64,2048]{1,0:T(8,128)(2,1)} collective-permute-done((bf16[64,2048]{1,0:T(8,128)(2,1)S(1)}, bf16[64,2048]{1,0:T(8,128)(2,1)}, u32[]{:S(2)}, u32[]{:S(2)}) %collective-permute-start.6) | collective-permute-done | bytes 262176 | tf_op jit(solution)/shard_map/ppermute | solution.py:140
  96.3 0.0 collective-permute-done.7
  96.3 3.2 %shard_map.47 = bf16[64,32,128]{2,1,0:T(8,128)(2,1)S(1)} custom-call(s32[2]{0:T(128)S(1)} %pad_add_fusion.where_ref, bf16[64,2048]{1,0:T(8,128)(2,1)S(1)} %bitcast.28, bf16[64,2048]{1,0:T(8,128)(2,1)} %collective-permute-done.refs_1_, bf16[64,2048]{1,0:T(8,128)(2,1)S(1)} %collective-permute-done.1.refs_2_, ...), custom_call_target="tpu_custom_call" | custom-call | flops 1073741824 | bytes 4194304 | tf_op jit(solution)/shard_map/pallas_call | solution.py:91
  99.5 24.8 %all_to_all.17.tiles_ref = bf16[64,32,128]{2,1,0:T(8,128)(2,1)S(1)} all-to-all(bf16[64,32,128]{2,1,0:T(8,128)(2,1)S(1)} %shard_map.47), channel_id=1, replica_groups=mesh['x_lo'=2,'y'=8,'core'=2,'z'=8,'x_hi'=2] {'x_lo','core','z','x_hi'}, dimensions={0} | all-to-all | bytes 1048576 | tf_op jit(solution)/shard_map/all_to_all | solution.py:149
  124.3 0.8 shard_map.48
  (1 shorter events, 0.0 us)
Async XLA Ops:
  0.0 35.3 %copy-start = (bf16[32,32]{1,0:T(8,128)(2,1)S(1)}, bf16[32,32]{1,0:T(8,128)(2,1)}, u32[]{:S(2)}) copy-start(bf16[32,32]{1,0:T(8,128)(2,1)} %param.5) | copy-start | bytes 6148
  0.0 1.1 copy-start.1
  1.1 0.7 copy-start.2
  52.4 43.9 %collective-permute-start.7 = (bf16[4,64,2048]{2,1,0:T(8,128)(2,1)S(1)}, bf16[4,64,2048]{2,1,0:T(8,128)(2,1)S(1)}, u32[]{:S(2)}, u32[]{:S(2)}) collective-permute-start(bf16[4,64,2048]{2,1,0:T(8,128)(2,1)S(1)} %all_to_all.16), channel_id=1, source_target_pairs={{0,16},{16,0},{1,17},{17,1},{2,18},{18,2},{3,19},{19,3},{4,20},{20... | collective-permute-start | bytes 3145736 | tf_op jit(solution)/shard_map/ppermute | solution.py:146
  54.5 16.1 %collective-permute-start.1 = (bf16[64,2048]{1,0:T(8,128)(2,1)S(1)}, bf16[64,2048]{1,0:T(8,128)(2,1)S(1)}, u32[]{:S(2)}, u32[]{:S(2)}) collective-permute-start(bf16[64,2048]{1,0:T(8,128)(2,1)S(1)} %bitcast.24), channel_id=1, source_target_pairs={{0,64},{32,96},{64,128},{96,160},{128,192},{160,224},{192,0},{224,... | collective-permute-start | bytes 786440 | tf_op jit(solution)/shard_map/ppermute | solution.py:136
  59.0 23.1 %collective-permute-start.4 = (bf16[64,2048]{1,0:T(8,128)(2,1)S(1)}, bf16[64,2048]{1,0:T(8,128)(2,1)S(1)}, u32[]{:S(2)}, u32[]{:S(2)}) collective-permute-start(bf16[64,2048]{1,0:T(8,128)(2,1)S(1)} %bitcast.25), channel_id=1, source_target_pairs={{0,192},{32,224},{64,0},{96,32},{128,64},{160,96},{192,128},{224,1... | collective-permute-start | bytes 786440 | tf_op jit(solution)/shard_map/ppermute | solution.py:137
  70.6 15.5 %collective-permute-start.2 = (bf16[64,2048]{1,0:T(8,128)(2,1)S(1)}, bf16[64,2048]{1,0:T(8,128)(2,1)S(1)}, u32[]{:S(2)}, u32[]{:S(2)}) collective-permute-start(bf16[64,2048]{1,0:T(8,128)(2,1)S(1)} %collective-permute-done.1.refs_2_), channel_id=1, source_target_pairs={{0,32},{32,64},{64,96},{96,128},{128,160},{160,192},{192,224},{224... | collective-permute-start | bytes 786440 | tf_op jit(solution)/shard_map/ppermute | solution.py:138
  76.3 11.8 %collective-permute-start.3 = (bf16[64,2048]{1,0:T(8,128)(2,1)S(1)}, bf16[64,2048]{1,0:T(8,128)(2,1)S(1)}, u32[]{:S(2)}, u32[]{:S(2)}) collective-permute-start(bf16[64,2048]{1,0:T(8,128)(2,1)S(1)} %bitcast.26), channel_id=1, source_target_pairs={{0,224},{32,0},{64,32},{96,64},{128,96},{160,128},{192,160},{224,1... | collective-permute-start | bytes 786440 | tf_op jit(solution)/shard_map/ppermute | solution.py:135
  79.0 10.8 %collective-permute-start = (bf16[64,2048]{1,0:T(8,128)(2,1)S(1)}, bf16[64,2048]{1,0:T(8,128)(2,1)}, u32[]{:S(2)}, u32[]{:S(2)}) collective-permute-start(bf16[64,2048]{1,0:T(8,128)(2,1)S(1)} %bitcast.27), channel_id=1, source_target_pairs={{0,32},{32,64},{64,96},{96,128},{128,160},{160,192},{192,224},{224... | collective-permute-start | bytes 786440 | tf_op jit(solution)/shard_map/ppermute | solution.py:134
  82.2 9.4 %collective-permute-start.5 = (bf16[64,2048]{1,0:T(8,128)(2,1)S(1)}, bf16[64,2048]{1,0:T(8,128)(2,1)}, u32[]{:S(2)}, u32[]{:S(2)}) collective-permute-start(bf16[64,2048]{1,0:T(8,128)(2,1)S(1)} %collective-permute-done.4.refs_5_), channel_id=1, source_target_pairs={{0,224},{32,0},{64,32},{96,64},{128,96},{160,128},{192,160},{224,1... | collective-permute-start | bytes 786440 | tf_op jit(solution)/shard_map/ppermute | solution.py:139
  86.1 10.2 %collective-permute-start.6 = (bf16[64,2048]{1,0:T(8,128)(2,1)S(1)}, bf16[64,2048]{1,0:T(8,128)(2,1)}, u32[]{:S(2)}, u32[]{:S(2)}) collective-permute-start(bf16[64,2048]{1,0:T(8,128)(2,1)S(1)} %collective-permute-done.2.refs_3_), channel_id=1, source_target_pairs={{0,32},{32,64},{64,96},{96,128},{128,160},{160,192},{192,224},{224... | collective-permute-start | bytes 786440 | tf_op jit(solution)/shard_map/ppermute | solution.py:140

commit v3 on v2

--- a/solution.py
+++ b/solution.py
@@ -13,7 +13,7 @@
 
 
 def ring(step):
-    return [(y, (y + step) % 8) for y in range(8)]
+    return [(y * 2 + c, (y + step * (1 - 2 * c)) % 8 * 2 + c) for y in range(8) for c in range(2)]
 
 
 def prepare_kernel(screen_ref, values_ref, density_ref, out_ref, kept, virtual):
@@ -63,13 +63,14 @@
         copies.append(pltpu.make_async_copy(source, target, done.at[len(copies)]))
         copies[-1].start()
 
+    sign = 1 - 2 * core
     for i, steps in enumerate((0, 1, 2, 3, -1, -2, -3, 4)):
-        at = lax.rem(y - steps + 8, 8)
+        at = lax.rem(y - sign * steps + 8, 8)
         bring(columns[i], left.at[pl.ds(pl.multiple_of(at * 64, 64), 64), :])
     for i in range(4):
         for blocks, owner in ((mine, core), (other, 1 - core)):
             at = i // 2 * 4 + owner * 2 + i % 2
-            bring(blocks.at[i], right.at[:, pl.ds(pl.multiple_of(at * 16, 16), 16), :])
+            right[:, pl.ds(pl.multiple_of(at * 16, 16), 16), :] = blocks[i]
     for copy in copies:
         copy.wait()
     for part_id in range(2):
@@ -91,12 +92,14 @@
     return pl.pallas_call(
         multiply_kernel,
         out_shape=jax.ShapeDtypeStruct((64, 32, 128), jnp.bfloat16),
-        in_specs=[pl.BlockSpec(memory_space=pltpu.SMEM)] + [pl.BlockSpec(memory_space=pl.ANY)] * 10,
+        in_specs=[pl.BlockSpec(memory_space=pltpu.SMEM)]
+        + [pl.BlockSpec(memory_space=pl.ANY)] * 8
+        + [pl.BlockSpec(memory_space=pltpu.VMEM)] * 2,
         out_specs=pl.BlockSpec(memory_space=pltpu.VMEM),
         scratch_shapes=[
             pltpu.VMEM((512, 2048), jnp.bfloat16),
             pltpu.VMEM((4, 128, 2048), jnp.bfloat16),
-            pltpu.SemaphoreType.DMA((16,)),
+            pltpu.SemaphoreType.DMA((8,)),
         ],
         compiler_params=pltpu.CompilerParams(vmem_limit_bytes=20 * 1024 * 1024),
         cost_estimate=pl.CostEstimate(flops=2 * 512 * 512 * 2048, bytes_accessed=4 << 20, transcendentals=0),
@@ -131,13 +134,13 @@
     got = lax.all_to_all(prepare(screen, integrals, virt_density), PLANE, 0, 0, tiled=True)
     own = unpack(got[:, :16])
     core = lax.axis_index("core")
-    up1 = lax.ppermute(own, "y", ring(1))
-    down1 = lax.ppermute(own, "y", ring(-1))
-    up2 = lax.ppermute(own, "y", ring(2))
-    down2 = lax.ppermute(own, "y", ring(-2))
-    up3 = lax.ppermute(up2, "y", ring(1))
-    down3 = lax.ppermute(down2, "y", ring(-1))
-    far = lax.ppermute(up3, "y", ring(1))
+    up1 = lax.ppermute(own, ("y", "core"), ring(1))
+    down1 = lax.ppermute(own, ("y", "core"), ring(-1))
+    up2 = lax.ppermute(own, ("y", "core"), ring(2))
+    down2 = lax.ppermute(own, ("y", "core"), ring(-2))
+    up3 = lax.ppermute(up2, ("y", "core"), ring(1))
+    down3 = lax.ppermute(down2, ("y", "core"), ring(-1))
+    far = lax.ppermute(up2, ("y", "core"), ring(2))
     columns = [own, up1, up2, up3, down1, down2, down3, far]
     virt_rows = unpack(got[:, 16:]).reshape(64, 32, 64)
     occupied = jnp.einsum("pms,ml->pls", virt_rows, occ_density, preferred_element_type=jnp.float32)

time: 126 us -> 121 us (0.960)
  starting transfers between devices: 27.4 us -> 23.7 us
    ppermute x7, starting transfers between devices: 25.5 us -> 21.8 us  [the longest x1 6.18 us: body(): down2 = lax.ppermute(own, ('y', 'core'), ring(-2))]
  transfers between devices with their start and end apart: 8 -> 8, of which waited for: 4 -> 5; matrix products, arithmetic and copies ran while one was open for 0% -> 0% of each run, Pallas kernels for 0% -> 0%
where the time goes in v3:
time: 121 us; the launch traced here: 120 us
  blocking collectives  73.2 us (60%)
  starting transfers between devices  23.7 us (20%)
  waiting for transfers between devices  15.1 us (12%)
  Pallas kernels  4.92 us (4%)
  local copies, waits for them, and re-layouts  2.88 us (2%)
    all_to_all x1, blocking collectives, body(): lax.all_to_all(prepare(screen, integrals, virt_density), PLANE, 0, 0, til...  32.2 us
    all_to_all x1, blocking collectives, body(): got = lax.all_to_all(tiles, PLANE, 0, 0, tiled=True)  24.8 us
    all_to_all x1, blocking collectives, body(): lax.all_to_all(jnp.broadcast_to(occupied, (4, 64, 2048)), XX, 0, 0, tiled...  16.2 us
    ppermute x1, starting transfers between devices, body(): down2 = lax.ppermute(own, ('y', 'core'), ring(-2))  6.18 us
    ppermute x1, waiting for transfers between devices, body(): far = lax.ppermute(up2, ('y', 'core'), ring(2))  6.05 us
    ppermute x1, starting transfers between devices, body(): down1 = lax.ppermute(own, ('y', 'core'), ring(-1))  5.25 us
    ppermute x1, waiting for transfers between devices, body(): down3 = lax.ppermute(down2, ('y', 'core'), ring(-1))  3.36 us
    pallas_call x1, Pallas kernels, multiply(): pl.pallas_call(multiply_kernel, out_shape=jax.ShapeDtypeStruct((64, 32, 1...  3.17 us
  transfers between devices with their start and end apart: 8, of which 5 were waited for; matrix products, arithmetic and copies ran while one was open for 0% of the time, Pallas kernels for 0%

profile of v3, /device:TPU:6, one launch (start us, length us, event | category | flops | bytes accessed | tf_op | source)
XLA Modules:
  0.0 120.3 jit_solution(8489686676737962980)
XLA Ops:
  0.0 0.0 copy-start
  0.0 0.0 copy-start.1
  0.0 1.1 reshape.21.values_ref
  1.1 0.0 copy-done.1
  1.1 0.0 copy-start.2
  1.1 0.7 copy-done.2
  1.8 1.0 shard_map.46
  2.8 32.2 %all_to_all.15 = bf16[64,32,128]{2,1,0:T(8,128)(2,1)S(1)} all-to-all(bf16[64,32,128]{2,1,0:T(8,128)(2,1)S(1)} %shard_map.46), channel_id=1, replica_groups=mesh['x_lo'=2,'y'=8,'core'=2,'z'=8,'x_hi'=2] {'x_lo','core','z','x_hi'}, dimensions={0} | all-to-all | bytes 1048576 | tf_op jit(solution)/shard_map/all_to_all | solution.py:134
  35.0 0.1 copy.6
  35.1 0.2 reshape_reshape.3
  35.3 0.0 copy-done
  35.3 0.3 fusion
  35.7 0.5 reshape.25
  36.2 0.1 broadcast_in_dim.3
  36.3 16.2 %all_to_all.16 = bf16[4,64,2048]{2,1,0:T(8,128)(2,1)S(1)} all-to-all(bf16[4,64,2048]{2,1,0:T(8,128)(2,1)S(1)} %broadcast_in_dim.3), channel_id=1, replica_groups=mesh['x_lo'=2,'y'=8,'core'=2,'z'=8,'x_hi'=2] {'x_lo','x_hi'}, dimensions={0} | all-to-all | bytes 2097152 | tf_op jit(solution)/shard_map/all_to_all | solution.py:148
  52.4 1.9 %collective-permute-start.7 = (bf16[4,64,2048]{2,1,0:T(8,128)(2,1)S(1)}, bf16[4,64,2048]{2,1,0:T(8,128)(2,1)S(1)}, u32[]{:S(2)}, u32[]{:S(2)}) collective-permute-start(bf16[4,64,2048]{2,1,0:T(8,128)(2,1)S(1)} %all_to_all.16), channel_id=1, source_target_pairs={{0,16},{16,0},{1,17},{17,1},{2,18},{18,2},{3,19},{19,3},{4,20},{20... | collective-permute-start | bytes 3145736 | tf_op jit(solution)/shard_map/ppermute | solution.py:149
  54.4 0.1 copy.5
  54.4 0.1 copy.12
  54.5 6.2 %collective-permute-start.4 = (bf16[64,2048]{1,0:T(8,128)(2,1)S(1)}, bf16[64,2048]{1,0:T(8,128)(2,1)S(1)}, u32[]{:S(2)}, u32[]{:S(2)}) collective-permute-start(bf16[64,2048]{1,0:T(8,128)(2,1)S(1)} %bitcast.24), channel_id=1, source_target_pairs={{0,192},{16,80},{32,224},{48,112},{64,0},{80,144},{96,32},{112,176... | collective-permute-start | bytes 786440 | tf_op jit(solution)/shard_map/ppermute | solution.py:140
  60.7 1.9 %collective-permute-start.1 = (bf16[64,2048]{1,0:T(8,128)(2,1)S(1)}, bf16[64,2048]{1,0:T(8,128)(2,1)S(1)}, u32[]{:S(2)}, u32[]{:S(2)}) collective-permute-start(bf16[64,2048]{1,0:T(8,128)(2,1)S(1)} %bitcast.25), channel_id=1, source_target_pairs={{0,64},{16,208},{32,96},{48,240},{64,128},{80,16},{96,160},{112,48... | collective-permute-start | bytes 786440 | tf_op jit(solution)/shard_map/ppermute | solution.py:139
  62.6 5.3 %collective-permute-start.3 = (bf16[64,2048]{1,0:T(8,128)(2,1)S(1)}, bf16[64,2048]{1,0:T(8,128)(2,1)S(1)}, u32[]{:S(2)}, u32[]{:S(2)}) collective-permute-start(bf16[64,2048]{1,0:T(8,128)(2,1)S(1)} %bitcast.26), channel_id=1, source_target_pairs={{0,224},{16,48},{32,0},{48,80},{64,32},{80,112},{96,64},{112,144},... | collective-permute-start | bytes 786440 | tf_op jit(solution)/shard_map/ppermute | solution.py:138
  67.9 1.9 %collective-permute-start = (bf16[64,2048]{1,0:T(8,128)(2,1)S(1)}, bf16[64,2048]{1,0:T(8,128)(2,1)S(1)}, u32[]{:S(2)}, u32[]{:S(2)}) collective-permute-start(bf16[64,2048]{1,0:T(8,128)(2,1)S(1)} %bitcast.27), channel_id=1, source_target_pairs={{0,32},{16,240},{32,64},{48,16},{64,96},{80,48},{96,128},{112,80},... | collective-permute-start | bytes 786440 | tf_op jit(solution)/shard_map/ppermute | solution.py:137
  69.8 2.4 %collective-permute-done.4.refs_5_ = bf16[64,2048]{1,0:T(8,128)(2,1)S(1)} collective-permute-done((bf16[64,2048]{1,0:T(8,128)(2,1)S(1)}, bf16[64,2048]{1,0:T(8,128)(2,1)S(1)}, u32[]{:S(2)}, u32[]{:S(2)}) %collective-permute-start.4) | collective-permute-done | bytes 262176 | tf_op jit(solution)/shard_map/ppermute | solution.py:140
  72.2 2.7 %collective-permute-start.5 = (bf16[64,2048]{1,0:T(8,128)(2,1)S(1)}, bf16[64,2048]{1,0:T(8,128)(2,1)}, u32[]{:S(2)}, u32[]{:S(2)}) collective-permute-start(bf16[64,2048]{1,0:T(8,128)(2,1)S(1)} %collective-permute-done.4.refs_5_), channel_id=1, source_target_pairs={{0,224},{16,48},{32,0},{48,80},{64,32},{80,112},{96,64},{112,144},... | collective-permute-start | bytes 786440 | tf_op jit(solution)/shard_map/ppermute | solution.py:142
  75.0 2.4 %collective-permute-done.1.refs_2_ = bf16[64,2048]{1,0:T(8,128)(2,1)S(1)} collective-permute-done((bf16[64,2048]{1,0:T(8,128)(2,1)S(1)}, bf16[64,2048]{1,0:T(8,128)(2,1)S(1)}, u32[]{:S(2)}, u32[]{:S(2)}) %collective-permute-start.1) | collective-permute-done | bytes 262176 | tf_op jit(solution)/shard_map/ppermute | solution.py:139
  77.3 1.9 %collective-permute-start.6 = (bf16[64,2048]{1,0:T(8,128)(2,1)S(1)}, bf16[64,2048]{1,0:T(8,128)(2,1)}, u32[]{:S(2)}, u32[]{:S(2)}) collective-permute-start(bf16[64,2048]{1,0:T(8,128)(2,1)S(1)} %collective-permute-done.1.refs_2_), channel_id=1, source_target_pairs={{0,64},{16,208},{32,96},{48,240},{64,128},{80,16},{96,160},{112,48... | collective-permute-start | bytes 786440 | tf_op jit(solution)/shard_map/ppermute | solution.py:143
  79.3 0.0 collective-permute-done.3.refs_4_
  79.3 1.9 %collective-permute-start.2 = (bf16[64,2048]{1,0:T(8,128)(2,1)S(1)}, bf16[64,2048]{1,0:T(8,128)(2,1)}, u32[]{:S(2)}, u32[]{:S(2)}) collective-permute-start(bf16[64,2048]{1,0:T(8,128)(2,1)S(1)} %collective-permute-done.1.refs_2_), channel_id=1, source_target_pairs={{0,32},{16,240},{32,64},{48,16},{64,96},{80,48},{96,128},{112,80},... | collective-permute-start | bytes 786440 | tf_op jit(solution)/shard_map/ppermute | solution.py:141
  81.2 0.1 pad_add_fusion.where_ref
  81.3 0.0 collective-permute-done.refs_1_
  81.3 3.4 %collective-permute-done.5.refs_6_ = bf16[64,2048]{1,0:T(8,128)(2,1)} collective-permute-done((bf16[64,2048]{1,0:T(8,128)(2,1)S(1)}, bf16[64,2048]{1,0:T(8,128)(2,1)}, u32[]{:S(2)}, u32[]{:S(2)}) %collective-permute-start.5) | collective-permute-done | bytes 262176 | tf_op jit(solution)/shard_map/ppermute | solution.py:142
  84.7 6.0 %collective-permute-done.6.refs_7_ = bf16[64,2048]{1,0:T(8,128)(2,1)} collective-permute-done((bf16[64,2048]{1,0:T(8,128)(2,1)S(1)}, bf16[64,2048]{1,0:T(8,128)(2,1)}, u32[]{:S(2)}, u32[]{:S(2)}) %collective-permute-start.6) | collective-permute-done | bytes 262176 | tf_op jit(solution)/shard_map/ppermute | solution.py:143
  90.7 0.8 collective-permute-done.2.refs_3_
  91.5 0.0 collective-permute-done.7
  91.5 3.2 %shard_map.47 = bf16[64,32,128]{2,1,0:T(8,128)(2,1)S(1)} custom-call(s32[2]{0:T(128)S(1)} %pad_add_fusion.where_ref, bf16[64,2048]{1,0:T(8,128)(2,1)S(1)} %bitcast.28, bf16[64,2048]{1,0:T(8,128)(2,1)S(1)} %collective-permute-done.refs_1_, bf16[64,2048]{1,0:T(8,128)(2,1)S(1)} %collective-permute-done.1.refs_2_, ...), custom_call_target="tpu_custom_call" | custom-call | flops 1073741824 | bytes 4194304 | tf_op jit(solution)/shard_map/pallas_call | solution.py:92
  94.7 24.8 %all_to_all.17.tiles_ref = bf16[64,32,128]{2,1,0:T(8,128)(2,1)S(1)} all-to-all(bf16[64,32,128]{2,1,0:T(8,128)(2,1)S(1)} %shard_map.47), channel_id=1, replica_groups=mesh['x_lo'=2,'y'=8,'core'=2,'z'=8,'x_hi'=2] {'x_lo','core','z','x_hi'}, dimensions={0} | all-to-all | bytes 1048576 | tf_op jit(solution)/shard_map/all_to_all | solution.py:152
  119.5 0.8 shard_map.48
  (1 shorter events, 0.0 us)
Async XLA Ops:
  0.0 35.3 %copy-start = (bf16[32,32]{1,0:T(8,128)(2,1)S(1)}, bf16[32,32]{1,0:T(8,128)(2,1)}, u32[]{:S(2)}) copy-start(bf16[32,32]{1,0:T(8,128)(2,1)} %param.5) | copy-start | bytes 6148
  0.0 1.1 copy-start.1
  1.1 0.7 copy-start.2
  52.4 39.1 %collective-permute-start.7 = (bf16[4,64,2048]{2,1,0:T(8,128)(2,1)S(1)}, bf16[4,64,2048]{2,1,0:T(8,128)(2,1)S(1)}, u32[]{:S(2)}, u32[]{:S(2)}) collective-permute-start(bf16[4,64,2048]{2,1,0:T(8,128)(2,1)S(1)} %all_to_all.16), channel_id=1, source_target_pairs={{0,16},{16,0},{1,17},{17,1},{2,18},{18,2},{3,19},{19,3},{4,20},{20... | collective-permute-start | bytes 3145736 | tf_op jit(solution)/shard_map/ppermute | solution.py:149
  54.5 17.7 %collective-permute-start.4 = (bf16[64,2048]{1,0:T(8,128)(2,1)S(1)}, bf16[64,2048]{1,0:T(8,128)(2,1)S(1)}, u32[]{:S(2)}, u32[]{:S(2)}) collective-permute-start(bf16[64,2048]{1,0:T(8,128)(2,1)S(1)} %bitcast.24), channel_id=1, source_target_pairs={{0,192},{16,80},{32,224},{48,112},{64,0},{80,144},{96,32},{112,176... | collective-permute-start | bytes 786440 | tf_op jit(solution)/shard_map/ppermute | solution.py:140
  60.7 16.6 %collective-permute-start.1 = (bf16[64,2048]{1,0:T(8,128)(2,1)S(1)}, bf16[64,2048]{1,0:T(8,128)(2,1)S(1)}, u32[]{:S(2)}, u32[]{:S(2)}) collective-permute-start(bf16[64,2048]{1,0:T(8,128)(2,1)S(1)} %bitcast.25), channel_id=1, source_target_pairs={{0,64},{16,208},{32,96},{48,240},{64,128},{80,16},{96,160},{112,48... | collective-permute-start | bytes 786440 | tf_op jit(solution)/shard_map/ppermute | solution.py:139
  62.6 16.6 %collective-permute-start.3 = (bf16[64,2048]{1,0:T(8,128)(2,1)S(1)}, bf16[64,2048]{1,0:T(8,128)(2,1)S(1)}, u32[]{:S(2)}, u32[]{:S(2)}) collective-permute-start(bf16[64,2048]{1,0:T(8,128)(2,1)S(1)} %bitcast.26), channel_id=1, source_target_pairs={{0,224},{16,48},{32,0},{48,80},{64,32},{80,112},{96,64},{112,144},... | collective-permute-start | bytes 786440 | tf_op jit(solution)/shard_map/ppermute | solution.py:138
  67.9 13.4 %collective-permute-start = (bf16[64,2048]{1,0:T(8,128)(2,1)S(1)}, bf16[64,2048]{1,0:T(8,128)(2,1)S(1)}, u32[]{:S(2)}, u32[]{:S(2)}) collective-permute-start(bf16[64,2048]{1,0:T(8,128)(2,1)S(1)} %bitcast.27), channel_id=1, source_target_pairs={{0,32},{16,240},{32,64},{48,16},{64,96},{80,48},{96,128},{112,80},... | collective-permute-start | bytes 786440 | tf_op jit(solution)/shard_map/ppermute | solution.py:137
  72.2 12.4 %collective-permute-start.5 = (bf16[64,2048]{1,0:T(8,128)(2,1)S(1)}, bf16[64,2048]{1,0:T(8,128)(2,1)}, u32[]{:S(2)}, u32[]{:S(2)}) collective-permute-start(bf16[64,2048]{1,0:T(8,128)(2,1)S(1)} %collective-permute-done.4.refs_5_), channel_id=1, source_target_pairs={{0,224},{16,48},{32,0},{48,80},{64,32},{80,112},{96,64},{112,144},... | collective-permute-start | bytes 786440 | tf_op jit(solution)/shard_map/ppermute | solution.py:142
  77.3 13.4 %collective-permute-start.6 = (bf16[64,2048]{1,0:T(8,128)(2,1)S(1)}, bf16[64,2048]{1,0:T(8,128)(2,1)}, u32[]{:S(2)}, u32[]{:S(2)}) collective-permute-start(bf16[64,2048]{1,0:T(8,128)(2,1)S(1)} %collective-permute-done.1.refs_2_), channel_id=1, source_target_pairs={{0,64},{16,208},{32,96},{48,240},{64,128},{80,16},{96,160},{112,48... | collective-permute-start | bytes 786440 | tf_op jit(solution)/shard_map/ppermute | solution.py:143
  79.3 12.3 %collective-permute-start.2 = (bf16[64,2048]{1,0:T(8,128)(2,1)S(1)}, bf16[64,2048]{1,0:T(8,128)(2,1)}, u32[]{:S(2)}, u32[]{:S(2)}) collective-permute-start(bf16[64,2048]{1,0:T(8,128)(2,1)S(1)} %collective-permute-done.1.refs_2_), channel_id=1, source_target_pairs={{0,32},{16,240},{32,64},{48,16},{64,96},{80,48},{96,128},{112,80},... | collective-permute-start | bytes 786440 | tf_op jit(solution)/shard_map/ppermute | solution.py:141

commit v4 on v3

--- a/solution.py
+++ b/solution.py
@@ -70,7 +70,7 @@
     for i in range(4):
         for blocks, owner in ((mine, core), (other, 1 - core)):
             at = i // 2 * 4 + owner * 2 + i % 2
-            right[:, pl.ds(pl.multiple_of(at * 16, 16), 16), :] = blocks[i]
+            bring(blocks.at[i], right.at[:, pl.ds(pl.multiple_of(at * 16, 16), 16), :])
     for copy in copies:
         copy.wait()
     for part_id in range(2):
@@ -92,14 +92,12 @@
     return pl.pallas_call(
         multiply_kernel,
         out_shape=jax.ShapeDtypeStruct((64, 32, 128), jnp.bfloat16),
-        in_specs=[pl.BlockSpec(memory_space=pltpu.SMEM)]
-        + [pl.BlockSpec(memory_space=pl.ANY)] * 8
-        + [pl.BlockSpec(memory_space=pltpu.VMEM)] * 2,
+        in_specs=[pl.BlockSpec(memory_space=pltpu.SMEM)] + [pl.BlockSpec(memory_space=pl.ANY)] * 10,
         out_specs=pl.BlockSpec(memory_space=pltpu.VMEM),
         scratch_shapes=[
             pltpu.VMEM((512, 2048), jnp.bfloat16),
             pltpu.VMEM((4, 128, 2048), jnp.bfloat16),
-            pltpu.SemaphoreType.DMA((8,)),
+            pltpu.SemaphoreType.DMA((16,)),
         ],
         compiler_params=pltpu.CompilerParams(vmem_limit_bytes=20 * 1024 * 1024),
         cost_estimate=pl.CostEstimate(flops=2 * 512 * 512 * 2048, bytes_accessed=4 << 20, transcendentals=0),

time: 121 us -> 121 us (level)
  no operation moved by 1% of the time
where the time goes in v4:
time: 121 us; the launch traced here: 120 us
  blocking collectives  73.2 us (60%)
  starting transfers between devices  23.7 us (20%)
  waiting for transfers between devices  15.1 us (12%)
  Pallas kernels  4.94 us (4%)
  local copies, waits for them, and re-layouts  2.88 us (2%)
    all_to_all x1, blocking collectives, body(): lax.all_to_all(prepare(screen, integrals, virt_density), PLANE, 0, 0, til...  32.2 us
    all_to_all x1, blocking collectives, body(): got = lax.all_to_all(tiles, PLANE, 0, 0, tiled=True)  24.8 us
    all_to_all x1, blocking collectives, body(): lax.all_to_all(jnp.broadcast_to(occupied, (4, 64, 2048)), XX, 0, 0, tiled...  16.2 us
    ppermute x1, starting transfers between devices, body(): down2 = lax.ppermute(own, ('y', 'core'), ring(-2))  6.18 us
    ppermute x1, waiting for transfers between devices, body(): far = lax.ppermute(up2, ('y', 'core'), ring(2))  6.05 us
    ppermute x1, starting transfers between devices, body(): down1 = lax.ppermute(own, ('y', 'core'), ring(-1))  5.25 us
    ppermute x1, waiting for transfers between devices, body(): down3 = lax.ppermute(down2, ('y', 'core'), ring(-1))  3.36 us
    pallas_call x1, Pallas kernels, multiply(): pl.pallas_call(multiply_kernel, out_shape=jax.ShapeDtypeStruct((64, 32, 1...  3.18 us
  transfers between devices with their start and end apart: 8, of which 5 were waited for; matrix products, arithmetic and copies ran while one was open for 0% of the time, Pallas kernels for 0%

profile of v4, /device:TPU:6, one launch (start us, length us, event | category | flops | bytes accessed | tf_op | source)
XLA Modules:
  0.0 120.4 jit_solution(8395935424755285996)
XLA Ops:
  0.0 0.0 copy-start
  0.0 0.0 copy-start.1
  0.0 1.1 reshape.21.values_ref
  1.1 0.0 copy-done.1
  1.1 0.0 copy-start.2
  1.1 0.7 copy-done.2
  1.8 1.0 shard_map.46
  2.8 32.2 %all_to_all.15 = bf16[64,32,128]{2,1,0:T(8,128)(2,1)S(1)} all-to-all(bf16[64,32,128]{2,1,0:T(8,128)(2,1)S(1)} %shard_map.46), channel_id=1, replica_groups=mesh['x_lo'=2,'y'=8,'core'=2,'z'=8,'x_hi'=2] {'x_lo','core','z','x_hi'}, dimensions={0} | all-to-all | bytes 1048576 | tf_op jit(solution)/shard_map/all_to_all | solution.py:132
  35.0 0.1 copy.6
  35.1 0.2 reshape_reshape.3
  35.3 0.0 copy-done
  35.3 0.3 fusion
  35.7 0.5 reshape.25
  36.2 0.1 broadcast_in_dim.3
  36.3 16.2 %all_to_all.16 = bf16[4,64,2048]{2,1,0:T(8,128)(2,1)S(1)} all-to-all(bf16[4,64,2048]{2,1,0:T(8,128)(2,1)S(1)} %broadcast_in_dim.3), channel_id=1, replica_groups=mesh['x_lo'=2,'y'=8,'core'=2,'z'=8,'x_hi'=2] {'x_lo','x_hi'}, dimensions={0} | all-to-all | bytes 2097152 | tf_op jit(solution)/shard_map/all_to_all | solution.py:146
  52.4 1.9 %collective-permute-start.7 = (bf16[4,64,2048]{2,1,0:T(8,128)(2,1)S(1)}, bf16[4,64,2048]{2,1,0:T(8,128)(2,1)S(1)}, u32[]{:S(2)}, u32[]{:S(2)}) collective-permute-start(bf16[4,64,2048]{2,1,0:T(8,128)(2,1)S(1)} %all_to_all.16), channel_id=1, source_target_pairs={{0,16},{16,0},{1,17},{17,1},{2,18},{18,2},{3,19},{19,3},{4,20},{20... | collective-permute-start | bytes 3145736 | tf_op jit(solution)/shard_map/ppermute | solution.py:147
  54.4 0.1 copy.5
  54.4 0.1 copy.12
  54.5 6.2 %collective-permute-start.4 = (bf16[64,2048]{1,0:T(8,128)(2,1)S(1)}, bf16[64,2048]{1,0:T(8,128)(2,1)S(1)}, u32[]{:S(2)}, u32[]{:S(2)}) collective-permute-start(bf16[64,2048]{1,0:T(8,128)(2,1)S(1)} %bitcast.24), channel_id=1, source_target_pairs={{0,192},{16,80},{32,224},{48,112},{64,0},{80,144},{96,32},{112,176... | collective-permute-start | bytes 786440 | tf_op jit(solution)/shard_map/ppermute | solution.py:138
  60.7 1.9 %collective-permute-start.1 = (bf16[64,2048]{1,0:T(8,128)(2,1)S(1)}, bf16[64,2048]{1,0:T(8,128)(2,1)S(1)}, u32[]{:S(2)}, u32[]{:S(2)}) collective-permute-start(bf16[64,2048]{1,0:T(8,128)(2,1)S(1)} %bitcast.25), channel_id=1, source_target_pairs={{0,64},{16,208},{32,96},{48,240},{64,128},{80,16},{96,160},{112,48... | collective-permute-start | bytes 786440 | tf_op jit(solution)/shard_map/ppermute | solution.py:137
  62.6 5.3 %collective-permute-start.3 = (bf16[64,2048]{1,0:T(8,128)(2,1)S(1)}, bf16[64,2048]{1,0:T(8,128)(2,1)S(1)}, u32[]{:S(2)}, u32[]{:S(2)}) collective-permute-start(bf16[64,2048]{1,0:T(8,128)(2,1)S(1)} %bitcast.26), channel_id=1, source_target_pairs={{0,224},{16,48},{32,0},{48,80},{64,32},{80,112},{96,64},{112,144},... | collective-permute-start | bytes 786440 | tf_op jit(solution)/shard_map/ppermute | solution.py:136
  67.9 1.9 %collective-permute-start = (bf16[64,2048]{1,0:T(8,128)(2,1)S(1)}, bf16[64,2048]{1,0:T(8,128)(2,1)S(1)}, u32[]{:S(2)}, u32[]{:S(2)}) collective-permute-start(bf16[64,2048]{1,0:T(8,128)(2,1)S(1)} %bitcast.27), channel_id=1, source_target_pairs={{0,32},{16,240},{32,64},{48,16},{64,96},{80,48},{96,128},{112,80},... | collective-permute-start | bytes 786440 | tf_op jit(solution)/shard_map/ppermute | solution.py:135
  69.8 2.4 %collective-permute-done.4.refs_5_ = bf16[64,2048]{1,0:T(8,128)(2,1)S(1)} collective-permute-done((bf16[64,2048]{1,0:T(8,128)(2,1)S(1)}, bf16[64,2048]{1,0:T(8,128)(2,1)S(1)}, u32[]{:S(2)}, u32[]{:S(2)}) %collective-permute-start.4) | collective-permute-done | bytes 262176 | tf_op jit(solution)/shard_map/ppermute | solution.py:138
  72.2 2.7 %collective-permute-start.5 = (bf16[64,2048]{1,0:T(8,128)(2,1)S(1)}, bf16[64,2048]{1,0:T(8,128)(2,1)}, u32[]{:S(2)}, u32[]{:S(2)}) collective-permute-start(bf16[64,2048]{1,0:T(8,128)(2,1)S(1)} %collective-permute-done.4.refs_5_), channel_id=1, source_target_pairs={{0,224},{16,48},{32,0},{48,80},{64,32},{80,112},{96,64},{112,144},... | collective-permute-start | bytes 786440 | tf_op jit(solution)/shard_map/ppermute | solution.py:140
  75.0 2.4 %collective-permute-done.1.refs_2_ = bf16[64,2048]{1,0:T(8,128)(2,1)S(1)} collective-permute-done((bf16[64,2048]{1,0:T(8,128)(2,1)S(1)}, bf16[64,2048]{1,0:T(8,128)(2,1)S(1)}, u32[]{:S(2)}, u32[]{:S(2)}) %collective-permute-start.1) | collective-permute-done | bytes 262176 | tf_op jit(solution)/shard_map/ppermute | solution.py:137
  77.3 1.9 %collective-permute-start.6 = (bf16[64,2048]{1,0:T(8,128)(2,1)S(1)}, bf16[64,2048]{1,0:T(8,128)(2,1)}, u32[]{:S(2)}, u32[]{:S(2)}) collective-permute-start(bf16[64,2048]{1,0:T(8,128)(2,1)S(1)} %collective-permute-done.1.refs_2_), channel_id=1, source_target_pairs={{0,64},{16,208},{32,96},{48,240},{64,128},{80,16},{96,160},{112,48... | collective-permute-start | bytes 786440 | tf_op jit(solution)/shard_map/ppermute | solution.py:141
  79.3 0.0 collective-permute-done.3.refs_4_
  79.3 1.9 %collective-permute-start.2 = (bf16[64,2048]{1,0:T(8,128)(2,1)S(1)}, bf16[64,2048]{1,0:T(8,128)(2,1)}, u32[]{:S(2)}, u32[]{:S(2)}) collective-permute-start(bf16[64,2048]{1,0:T(8,128)(2,1)S(1)} %collective-permute-done.1.refs_2_), channel_id=1, source_target_pairs={{0,32},{16,240},{32,64},{48,16},{64,96},{80,48},{96,128},{112,80},... | collective-permute-start | bytes 786440 | tf_op jit(solution)/shard_map/ppermute | solution.py:139
  81.2 0.1 pad_add_fusion.where_ref
  81.3 0.0 collective-permute-done.refs_1_
  81.3 3.4 %collective-permute-done.5.refs_6_ = bf16[64,2048]{1,0:T(8,128)(2,1)} collective-permute-done((bf16[64,2048]{1,0:T(8,128)(2,1)S(1)}, bf16[64,2048]{1,0:T(8,128)(2,1)}, u32[]{:S(2)}, u32[]{:S(2)}) %collective-permute-start.5) | collective-permute-done | bytes 262176 | tf_op jit(solution)/shard_map/ppermute | solution.py:140
  84.7 6.0 %collective-permute-done.6.refs_7_ = bf16[64,2048]{1,0:T(8,128)(2,1)} collective-permute-done((bf16[64,2048]{1,0:T(8,128)(2,1)S(1)}, bf16[64,2048]{1,0:T(8,128)(2,1)}, u32[]{:S(2)}, u32[]{:S(2)}) %collective-permute-start.6) | collective-permute-done | bytes 262176 | tf_op jit(solution)/shard_map/ppermute | solution.py:141
  90.7 0.8 collective-permute-done.2.refs_3_
  91.5 0.0 collective-permute-done.7
  91.5 3.2 %shard_map.47 = bf16[64,32,128]{2,1,0:T(8,128)(2,1)S(1)} custom-call(s32[2]{0:T(128)S(1)} %pad_add_fusion.where_ref, bf16[64,2048]{1,0:T(8,128)(2,1)S(1)} %bitcast.28, bf16[64,2048]{1,0:T(8,128)(2,1)S(1)} %collective-permute-done.refs_1_, bf16[64,2048]{1,0:T(8,128)(2,1)S(1)} %collective-permute-done.1.refs_2_, ...), custom_call_target="tpu_custom_call" | custom-call | flops 1073741824 | bytes 4194304 | tf_op jit(solution)/shard_map/pallas_call | solution.py:92
  94.7 24.8 %all_to_all.17.tiles_ref = bf16[64,32,128]{2,1,0:T(8,128)(2,1)S(1)} all-to-all(bf16[64,32,128]{2,1,0:T(8,128)(2,1)S(1)} %shard_map.47), channel_id=1, replica_groups=mesh['x_lo'=2,'y'=8,'core'=2,'z'=8,'x_hi'=2] {'x_lo','core','z','x_hi'}, dimensions={0} | all-to-all | bytes 1048576 | tf_op jit(solution)/shard_map/all_to_all | solution.py:150
  119.6 0.8 shard_map.48
  (1 shorter events, 0.0 us)
Async XLA Ops:
  0.0 35.3 %copy-start = (bf16[32,32]{1,0:T(8,128)(2,1)S(1)}, bf16[32,32]{1,0:T(8,128)(2,1)}, u32[]{:S(2)}) copy-start(bf16[32,32]{1,0:T(8,128)(2,1)} %param.5) | copy-start | bytes 6148
  0.0 1.1 copy-start.1
  1.1 0.7 copy-start.2
  52.4 39.1 %collective-permute-start.7 = (bf16[4,64,2048]{2,1,0:T(8,128)(2,1)S(1)}, bf16[4,64,2048]{2,1,0:T(8,128)(2,1)S(1)}, u32[]{:S(2)}, u32[]{:S(2)}) collective-permute-start(bf16[4,64,2048]{2,1,0:T(8,128)(2,1)S(1)} %all_to_all.16), channel_id=1, source_target_pairs={{0,16},{16,0},{1,17},{17,1},{2,18},{18,2},{3,19},{19,3},{4,20},{20... | collective-permute-start | bytes 3145736 | tf_op jit(solution)/shard_map/ppermute | solution.py:147
  54.5 17.7 %collective-permute-start.4 = (bf16[64,2048]{1,0:T(8,128)(2,1)S(1)}, bf16[64,2048]{1,0:T(8,128)(2,1)S(1)}, u32[]{:S(2)}, u32[]{:S(2)}) collective-permute-start(bf16[64,2048]{1,0:T(8,128)(2,1)S(1)} %bitcast.24), channel_id=1, source_target_pairs={{0,192},{16,80},{32,224},{48,112},{64,0},{80,144},{96,32},{112,176... | collective-permute-start | bytes 786440 | tf_op jit(solution)/shard_map/ppermute | solution.py:138
  60.7 16.6 %collective-permute-start.1 = (bf16[64,2048]{1,0:T(8,128)(2,1)S(1)}, bf16[64,2048]{1,0:T(8,128)(2,1)S(1)}, u32[]{:S(2)}, u32[]{:S(2)}) collective-permute-start(bf16[64,2048]{1,0:T(8,128)(2,1)S(1)} %bitcast.25), channel_id=1, source_target_pairs={{0,64},{16,208},{32,96},{48,240},{64,128},{80,16},{96,160},{112,48... | collective-permute-start | bytes 786440 | tf_op jit(solution)/shard_map/ppermute | solution.py:137
  62.6 16.6 %collective-permute-start.3 = (bf16[64,2048]{1,0:T(8,128)(2,1)S(1)}, bf16[64,2048]{1,0:T(8,128)(2,1)S(1)}, u32[]{:S(2)}, u32[]{:S(2)}) collective-permute-start(bf16[64,2048]{1,0:T(8,128)(2,1)S(1)} %bitcast.26), channel_id=1, source_target_pairs={{0,224},{16,48},{32,0},{48,80},{64,32},{80,112},{96,64},{112,144},... | collective-permute-start | bytes 786440 | tf_op jit(solution)/shard_map/ppermute | solution.py:136
  67.9 13.4 %collective-permute-start = (bf16[64,2048]{1,0:T(8,128)(2,1)S(1)}, bf16[64,2048]{1,0:T(8,128)(2,1)S(1)}, u32[]{:S(2)}, u32[]{:S(2)}) collective-permute-start(bf16[64,2048]{1,0:T(8,128)(2,1)S(1)} %bitcast.27), channel_id=1, source_target_pairs={{0,32},{16,240},{32,64},{48,16},{64,96},{80,48},{96,128},{112,80},... | collective-permute-start | bytes 786440 | tf_op jit(solution)/shard_map/ppermute | solution.py:135
  72.2 12.4 %collective-permute-start.5 = (bf16[64,2048]{1,0:T(8,128)(2,1)S(1)}, bf16[64,2048]{1,0:T(8,128)(2,1)}, u32[]{:S(2)}, u32[]{:S(2)}) collective-permute-start(bf16[64,2048]{1,0:T(8,128)(2,1)S(1)} %collective-permute-done.4.refs_5_), channel_id=1, source_target_pairs={{0,224},{16,48},{32,0},{48,80},{64,32},{80,112},{96,64},{112,144},... | collective-permute-start | bytes 786440 | tf_op jit(solution)/shard_map/ppermute | solution.py:140
  77.3 13.4 %collective-permute-start.6 = (bf16[64,2048]{1,0:T(8,128)(2,1)S(1)}, bf16[64,2048]{1,0:T(8,128)(2,1)}, u32[]{:S(2)}, u32[]{:S(2)}) collective-permute-start(bf16[64,2048]{1,0:T(8,128)(2,1)S(1)} %collective-permute-done.1.refs_2_), channel_id=1, source_target_pairs={{0,64},{16,208},{32,96},{48,240},{64,128},{80,16},{96,160},{112,48... | collective-permute-start | bytes 786440 | tf_op jit(solution)/shard_map/ppermute | solution.py:141
  79.3 12.3 %collective-permute-start.2 = (bf16[64,2048]{1,0:T(8,128)(2,1)S(1)}, bf16[64,2048]{1,0:T(8,128)(2,1)}, u32[]{:S(2)}, u32[]{:S(2)}) collective-permute-start(bf16[64,2048]{1,0:T(8,128)(2,1)S(1)} %collective-permute-done.1.refs_2_), channel_id=1, source_target_pairs={{0,32},{16,240},{32,64},{48,16},{64,96},{80,48},{96,128},{112,80},... | collective-permute-start | bytes 786440 | tf_op jit(solution)/shard_map/ppermute | solution.py:139
